TPU v7x, 32 devices: a whole 2x2x4 slice. The times are simulated.
32 devices in a mesh: dev: 2 (over x), sa: 16 (over z, y, core).
Axes of the slice: x: 2, y: 2, z: 4, core: 2. Of those that a mesh axis runs over, the one named last changes fastest.
Arguments:
- patches: bfloat16 [8, 1024, 1152], P('dev', 'sa'), may hold values from -6 to 6
- patch_mask: int32 [8, 1024], P('dev', 'sa'), may hold values from 0 to 1, as said below
- cotangent: bfloat16 [8, 1024, 1152], P('dev', 'sa'), may hold values from -6 to 6
- w_qkv: bfloat16 [1152, 3456], P('sa', 'dev'), may hold values from -0.1875 to 0.1875
- w_out: bfloat16 [1152, 1152], P('sa', 'dev'), may hold values from -0.75 to 0.75
- w_up: bfloat16 [1152, 4304], P('sa', 'dev'), may hold values from -0.1875 to 0.1875
- w_down: bfloat16 [1152, 4304], P('sa', 'dev'), may hold values from -0.125 to 0.125
- gain_one: bfloat16 [1, 1152], P(None, 'dev'), may hold values from 0.25 to 1.75
- shift_one: bfloat16 [1, 1152], P(None, 'dev'), may hold values from -4 to 4
- gain_two: bfloat16 [1, 1152], P(None, 'dev'), may hold values from 0.25 to 1.75
- shift_two: bfloat16 [1, 1152], P(None, 'dev'), may hold values from -4 to 4
- bias_query: bfloat16 [1, 1152], P(None, 'dev'), may hold values from -4 to 4
- bias_value: bfloat16 [1, 1152], P(None, 'dev'), may hold values from -4 to 4
- bias_out: bfloat16 [1, 1152], P(None, 'dev'), may hold values from -4 to 4
- bias_up: bfloat16 [1, 4304], P(None, 'dev'), may hold values from -4 to 4
- bias_down: bfloat16 [1, 1152], P(None, 'dev'), may hold values from -4 to 4
Outputs:
- result: bfloat16 [8, 1024, 1152], P('dev', 'sa')
- grad_patches: bfloat16 [8, 1024, 1152], P('dev', 'sa')
- grad_w_qkv: float32 [1152, 3456], P('sa', 'dev')
- grad_w_out: float32 [1152, 1152], P('sa', 'dev')
- grad_w_up: float32 [1152, 4304], P('sa', 'dev')
- grad_w_down: float32 [1152, 4304], P('sa', 'dev')
- grad_gain_one: float32 [1, 1152], P(None, 'dev')
- grad_shift_one: float32 [1, 1152], P(None, 'dev')
- grad_gain_two: float32 [1, 1152], P(None, 'dev')
- grad_shift_two: float32 [1, 1152], P(None, 'dev')
- grad_bias_query: float32 [1, 1152], P(None, 'dev')
- grad_bias_value: float32 [1, 1152], P(None, 'dev')
- grad_bias_out: float32 [1, 1152], P(None, 'dev')
- grad_bias_up: float32 [1, 4304], P(None, 'dev')
- grad_bias_down: float32 [1, 1152], P(None, 'dev')
Inputs may be any that keep to these rules, and one draw needn't show every extreme that they name: `patch_mask`: each image's ones are its first patches, 256 of them or more.
All inputs are finite; a program needn't handle non-finite values.
Results may differ from a plain program's by a relative error of at most 0.018.
Values may be sent and summed in bfloat16 or wider, within the bound.
No kernel may reach another device: no remote copies, remote signals or barrier semaphores. Data moves between devices by JAX's collectives and lax.ppermute only.
A program may use at most 256 MiB of HBM per device.

v0:
```python
import jax
import jax.numpy as jnp
from jax import lax
from jax.sharding import PartitionSpec as P

HEADS = 16
HEAD_DIM = 72
MICRO = 4


def normalize(values, gain, shift):
    centre = values - jnp.mean(values, axis=-1, keepdims=True)
    spread = jnp.mean(centre * centre, axis=-1, keepdims=True)
    return centre * lax.rsqrt(spread + 1e-06) * gain + shift


def gelu_tanh(values):
    return jax.nn.gelu(values, approximate=True)


def mat_rows(left, right):
    return lax.dot_general(
        left, right, (((0,), (0,)), ((), ())), preferred_element_type=jnp.float32
    )


def mat_last(left, right):
    return lax.dot_general(
        left, right, (((1,), (1,)), ((), ())), preferred_element_type=jnp.float32
    )


def score_block(query, all_kv, all_valid, width):
    images = all_kv.shape[0]
    seq_len = all_kv.shape[1]
    q_heads = query.reshape(images, -1, HEADS, HEAD_DIM)
    key_heads = all_kv[:, :, :width].reshape(images, seq_len, HEADS, HEAD_DIM)
    raw = jnp.einsum("iqhd,ikhd->ihqk", q_heads, key_heads, preferred_element_type=jnp.float32)
    raw = raw * HEAD_DIM ** (-0.5)
    return jnp.where(all_valid[:, None, None, :] > 0.5, raw, -1e30)


def per_device(
    patches,
    patch_mask,
    cotangent,
    w_qkv,
    w_out,
    w_up,
    w_down,
    gain_one,
    shift_one,
    gain_two,
    shift_two,
    bias_query,
    bias_value,
    bias_out,
    bias_up,
    bias_down,
):
    width = patches.shape[2]
    local_tokens = patches.shape[1]
    per_micro = patches.shape[0] // MICRO
    row_count = per_micro * local_tokens
    scale = HEAD_DIM ** (-0.5)
    row_parts = (
        lax.all_gather(w_qkv, "sa", axis=0, tiled=True),
        lax.all_gather(w_out, "sa", axis=0, tiled=True),
        lax.all_gather(w_up, "sa", axis=0, tiled=True),
        lax.all_gather(w_down, "sa", axis=0, tiled=True),
    )
    gathered = (
        lax.all_gather(row_parts[0], "dev", axis=1, tiled=True),
        lax.all_gather(row_parts[1], "dev", axis=1, tiled=True),
        lax.all_gather(row_parts[2], "dev", axis=1, tiled=True),
        lax.all_gather(row_parts[3], "dev", axis=1, tiled=True),
        lax.all_gather(gain_one, "dev", axis=1, tiled=True),
        lax.all_gather(shift_one, "dev", axis=1, tiled=True),
        lax.all_gather(gain_two, "dev", axis=1, tiled=True),
        lax.all_gather(shift_two, "dev", axis=1, tiled=True),
        lax.all_gather(bias_query, "dev", axis=1, tiled=True),
        lax.all_gather(bias_value, "dev", axis=1, tiled=True),
        lax.all_gather(bias_out, "dev", axis=1, tiled=True),
        lax.all_gather(bias_up, "dev", axis=1, tiled=True),
        lax.all_gather(bias_down, "dev", axis=1, tiled=True),
    )
    full_qkv, full_out, full_up, full_down = (gathered[0], gathered[1], gathered[2], gathered[3])
    vectors = [item.astype(jnp.float32)[0] for item in gathered[4:]]
    gain_first, shift_first, gain_second, shift_second = (
        vectors[0],
        vectors[1],
        vectors[2],
        vectors[3],
    )
    query_bias, value_bias, out_bias, up_bias, down_bias = (
        vectors[4],
        vectors[5],
        vectors[6],
        vectors[7],
        vectors[8],
    )
    qkv_bias = jnp.concatenate([query_bias, jnp.zeros((width,), jnp.float32), value_bias])
    outputs = []
    kept = []
    for micro_step in range(MICRO):
        begin = micro_step * per_micro
        inputs = patches[begin : begin + per_micro].astype(jnp.float32).reshape(row_count, width)
        normed_one = normalize(inputs, gain_first, shift_first).astype(jnp.bfloat16)
        projected = (
            jnp.dot(normed_one, full_qkv, preferred_element_type=jnp.float32) + qkv_bias
        ).astype(jnp.bfloat16)
        query = projected[:, :width]
        key_value = projected[:, width:].reshape(per_micro, local_tokens, 2 * width)
        valid = patch_mask[begin : begin + per_micro].astype(jnp.bfloat16)
        all_kv, all_valid = (
            lax.all_gather(key_value, "sa", axis=1, tiled=True),
            lax.all_gather(valid, "sa", axis=1, tiled=True),
        )
        seq_len = all_kv.shape[1]
        scores = score_block(query, all_kv, all_valid, width)
        peak = jnp.max(scores, axis=-1, keepdims=True)
        expo = jnp.exp(scores - peak)
        total = jnp.sum(expo, axis=-1, keepdims=True)
        log_total = peak + jnp.log(total)
        probs = (expo / total).astype(jnp.bfloat16)
        value_heads = all_kv[:, :, width:].reshape(per_micro, seq_len, HEADS, HEAD_DIM)
        attended = jnp.einsum(
            "ihqk,ikhd->iqhd", probs, value_heads, preferred_element_type=jnp.float32
        )
        attended = attended.reshape(row_count, width).astype(jnp.bfloat16)
        middle = inputs + jnp.dot(attended, full_out, preferred_element_type=jnp.float32) + out_bias
        normed_two = normalize(middle, gain_second, shift_second).astype(jnp.bfloat16)
        hidden_pre = jnp.dot(normed_two, full_up, preferred_element_type=jnp.float32) + up_bias
        activated = gelu_tanh(hidden_pre).astype(jnp.bfloat16)
        mlp_out = mat_last(activated, full_down) + down_bias
        outputs.append(
            (middle + mlp_out).astype(jnp.bfloat16).reshape(per_micro, local_tokens, width)
        )
        kept.append(
            (
                inputs,
                normed_one,
                query,
                key_value,
                valid,
                all_kv,
                all_valid,
                log_total,
                attended,
                middle,
                normed_two,
                hidden_pre,
                activated,
            )
        )
    rows_back = (
        lax.all_gather(w_qkv, "sa", axis=0, tiled=True),
        lax.all_gather(w_out, "sa", axis=0, tiled=True),
        lax.all_gather(w_up, "sa", axis=0, tiled=True),
        lax.all_gather(w_down, "sa", axis=0, tiled=True),
    )
    again = (
        lax.all_gather(rows_back[0], "dev", axis=1, tiled=True),
        lax.all_gather(rows_back[1], "dev", axis=1, tiled=True),
        lax.all_gather(rows_back[2], "dev", axis=1, tiled=True),
        lax.all_gather(rows_back[3], "dev", axis=1, tiled=True),
        lax.all_gather(gain_one, "dev", axis=1, tiled=True),
        lax.all_gather(shift_one, "dev", axis=1, tiled=True),
        lax.all_gather(gain_two, "dev", axis=1, tiled=True),
        lax.all_gather(shift_two, "dev", axis=1, tiled=True),
        lax.all_gather(bias_query, "dev", axis=1, tiled=True),
        lax.all_gather(bias_value, "dev", axis=1, tiled=True),
        lax.all_gather(bias_out, "dev", axis=1, tiled=True),
        lax.all_gather(bias_up, "dev", axis=1, tiled=True),
        lax.all_gather(bias_down, "dev", axis=1, tiled=True),
    )
    back_qkv, back_out, back_up, back_down = (again[0], again[1], again[2], again[3])
    back_vectors = [item.astype(jnp.float32)[0] for item in again[4:]]
    back_gain_first, back_shift_first = (back_vectors[0], back_vectors[1])
    back_gain_second, back_shift_second = (back_vectors[2], back_vectors[3])
    acc_qkv = jnp.zeros(back_qkv.shape, jnp.float32)
    acc_out = jnp.zeros(back_out.shape, jnp.float32)
    acc_up = jnp.zeros(back_up.shape, jnp.float32)
    acc_down = jnp.zeros(back_down.shape, jnp.float32)
    ff_width = back_up.shape[1]
    acc_vectors = [jnp.zeros((width,), jnp.float32) for index_value in range(7)] + [
        jnp.zeros((ff_width,), jnp.float32),
        jnp.zeros((width,), jnp.float32),
    ]
    grad_inputs = []
    for micro_step in range(MICRO):
        begin = micro_step * per_micro
        (
            inputs,
            normed_one,
            query,
            key_value,
            valid,
            all_kv,
            all_valid,
            log_total,
            attended,
            middle,
            normed_two,
            hidden_pre,
            activated,
        ) = kept[micro_step]
        seq_len = all_kv.shape[1]
        grad_out = (
            cotangent[begin : begin + per_micro].astype(jnp.float32).reshape(row_count, width)
        )
        grad_mlp = grad_out.astype(jnp.bfloat16)
        acc_down = acc_down + mat_rows(grad_mlp, activated)
        grad_act = jnp.dot(grad_mlp, back_down, preferred_element_type=jnp.float32)
        gelu_pull = jax.vjp(gelu_tanh, hidden_pre)[1]
        grad_hidden = gelu_pull(grad_act)[0].astype(jnp.bfloat16)
        acc_up = acc_up + mat_rows(normed_two, grad_hidden)
        grad_normed_two = mat_last(grad_hidden, back_up)
        norm_pull = jax.vjp(normalize, middle, back_gain_second, back_shift_second)[1]
        grad_middle_part, grad_gain_second, grad_shift_second = norm_pull(grad_normed_two)
        grad_middle = grad_out + grad_middle_part
        grad_branch = grad_middle.astype(jnp.bfloat16)
        acc_out = acc_out + mat_rows(attended, grad_branch)
        grad_att = mat_last(grad_branch, back_out).astype(jnp.bfloat16)
        grad_att_heads = grad_att.reshape(per_micro, local_tokens, HEADS, HEAD_DIM)
        scores = score_block(query, all_kv, all_valid, width)
        probs_full = jnp.exp(scores - log_total)
        probs = probs_full.astype(jnp.bfloat16)
        q_heads = query.reshape(per_micro, local_tokens, HEADS, HEAD_DIM)
        key_heads = all_kv[:, :, :width].reshape(per_micro, seq_len, HEADS, HEAD_DIM)
        value_heads = all_kv[:, :, width:].reshape(per_micro, seq_len, HEADS, HEAD_DIM)
        grad_probs = jnp.einsum(
            "iqhd,ikhd->ihqk", grad_att_heads, value_heads, preferred_element_type=jnp.float32
        )
        row_terms = jnp.sum(grad_probs * probs_full, axis=-1, keepdims=True)
        grad_scores = (probs_full * (grad_probs - row_terms)).astype(jnp.bfloat16)
        grad_query = (
            jnp.einsum(
                "ihqk,ikhd->iqhd", grad_scores, key_heads, preferred_element_type=jnp.float32
            )
            * scale
        )
        grad_value = jnp.einsum(
            "ihqk,iqhd->ikhd", probs, grad_att_heads, preferred_element_type=jnp.float32
        )
        grad_key = (
            jnp.einsum("ihqk,iqhd->ikhd", grad_scores, q_heads, preferred_element_type=jnp.float32)
            * scale
        )
        grad_kv_part = jnp.concatenate(
            [
                grad_key.reshape(per_micro, seq_len, width),
                grad_value.reshape(per_micro, seq_len, width),
            ],
            axis=2,
        )
        grad_kv = lax.psum_scatter(
            grad_kv_part.astype(jnp.bfloat16), "sa", scatter_dimension=1, tiled=True
        ).astype(jnp.float32)
        grad_proj = jnp.concatenate(
            [grad_query.reshape(row_count, width), grad_kv.reshape(row_count, 2 * width)], axis=1
        ).astype(jnp.bfloat16)
        acc_qkv = acc_qkv + mat_rows(normed_one, grad_proj)
        grad_normed_one = mat_last(grad_proj, back_qkv)
        first_pull = jax.vjp(normalize, inputs, back_gain_first, back_shift_first)[1]
        grad_in_part, grad_gain_first, grad_shift_first = first_pull(grad_normed_one)
        grad_inputs.append(
            (grad_middle + grad_in_part)
            .astype(jnp.bfloat16)
            .reshape(per_micro, local_tokens, width)
        )
        proj_sums = jnp.sum(grad_proj.astype(jnp.float32), axis=0)
        terms = [
            grad_gain_first,
            grad_shift_first,
            grad_gain_second,
            grad_shift_second,
            proj_sums[:width],
            proj_sums[2 * width :],
            jnp.sum(grad_branch.astype(jnp.float32), axis=0),
            jnp.sum(grad_hidden.astype(jnp.float32), axis=0),
            jnp.sum(grad_mlp.astype(jnp.float32), axis=0),
        ]
        acc_vectors = [held + fresh for held, fresh in zip(acc_vectors, terms)]
    row_sums = (
        lax.psum_scatter(
            acc_qkv.astype(jnp.bfloat16), "sa", scatter_dimension=0, tiled=True
        ).astype(jnp.float32),
        lax.psum_scatter(
            acc_out.astype(jnp.bfloat16), "sa", scatter_dimension=0, tiled=True
        ).astype(jnp.float32),
        lax.psum_scatter(acc_up.astype(jnp.bfloat16), "sa", scatter_dimension=0, tiled=True).astype(
            jnp.float32
        ),
        lax.psum_scatter(
            acc_down.astype(jnp.bfloat16), "sa", scatter_dimension=0, tiled=True
        ).astype(jnp.float32),
    )
    flat_vectors = [item[None, :] for item in acc_vectors]
    column_sums = (
        lax.psum_scatter(
            row_sums[0].astype(jnp.bfloat16), "dev", scatter_dimension=1, tiled=True
        ).astype(jnp.float32),
        lax.psum_scatter(
            row_sums[1].astype(jnp.bfloat16), "dev", scatter_dimension=1, tiled=True
        ).astype(jnp.float32),
        lax.psum_scatter(
            row_sums[2].astype(jnp.bfloat16), "dev", scatter_dimension=1, tiled=True
        ).astype(jnp.float32),
        lax.psum_scatter(
            row_sums[3].astype(jnp.bfloat16), "dev", scatter_dimension=1, tiled=True
        ).astype(jnp.float32),
        lax.psum_scatter(
            flat_vectors[0].astype(jnp.bfloat16), "dev", scatter_dimension=1, tiled=True
        ).astype(jnp.float32),
        lax.psum_scatter(
            flat_vectors[1].astype(jnp.bfloat16), "dev", scatter_dimension=1, tiled=True
        ).astype(jnp.float32),
        lax.psum_scatter(
            flat_vectors[2].astype(jnp.bfloat16), "dev", scatter_dimension=1, tiled=True
        ).astype(jnp.float32),
        lax.psum_scatter(
            flat_vectors[3].astype(jnp.bfloat16), "dev", scatter_dimension=1, tiled=True
        ).astype(jnp.float32),
        lax.psum_scatter(
            flat_vectors[4].astype(jnp.bfloat16), "dev", scatter_dimension=1, tiled=True
        ).astype(jnp.float32),
        lax.psum_scatter(
            flat_vectors[5].astype(jnp.bfloat16), "dev", scatter_dimension=1, tiled=True
        ).astype(jnp.float32),
        lax.psum_scatter(
            flat_vectors[6].astype(jnp.bfloat16), "dev", scatter_dimension=1, tiled=True
        ).astype(jnp.float32),
        lax.psum_scatter(
            flat_vectors[7].astype(jnp.bfloat16), "dev", scatter_dimension=1, tiled=True
        ).astype(jnp.float32),
        lax.psum_scatter(
            flat_vectors[8].astype(jnp.bfloat16), "dev", scatter_dimension=1, tiled=True
        ).astype(jnp.float32),
    )
    summed = lax.psum(
        (
            column_sums[4],
            column_sums[5],
            column_sums[6],
            column_sums[7],
            column_sums[8],
            column_sums[9],
            column_sums[10],
            column_sums[11],
            column_sums[12],
        ),
        "sa",
    )
    result = jnp.concatenate(outputs, axis=0)
    grad_patches = jnp.concatenate(grad_inputs, axis=0)
    return (
        result,
        grad_patches,
        column_sums[0],
        column_sums[1],
        column_sums[2],
        column_sums[3],
        summed[0],
        summed[1],
        summed[2],
        summed[3],
        summed[4],
        summed[5],
        summed[6],
        summed[7],
        summed[8],
    )


def solution(mesh):
    placed = (
        P("dev", "sa", None),
        P("dev", "sa"),
        P("dev", "sa", None),
        P("sa", "dev"),
        P("sa", "dev"),
        P("sa", "dev"),
        P("sa", "dev"),
        P(None, "dev"),
        P(None, "dev"),
        P(None, "dev"),
        P(None, "dev"),
        P(None, "dev"),
        P(None, "dev"),
        P(None, "dev"),
        P(None, "dev"),
        P(None, "dev"),
    )
    return jax.shard_map(
        per_device,
        mesh=mesh,
        in_specs=placed,
        out_specs=(
            P("dev", "sa", None),
            P("dev", "sa", None),
            P("sa", "dev"),
            P("sa", "dev"),
            P("sa", "dev"),
            P("sa", "dev"),
            P(None, "dev"),
            P(None, "dev"),
            P(None, "dev"),
            P(None, "dev"),
            P(None, "dev"),
            P(None, "dev"),
            P(None, "dev"),
            P(None, "dev"),
            P(None, "dev"),
        ),
        check_vma=False,
    )
```

profile of v0, /device:TPU:0, one launch (start us, length us, event | category | flops | bytes accessed | tf_op | source)
XLA Modules:
  0.0 1915.4 jit_solution(13595690874956938875)
XLA Ops:
  8.0 55.3 %all-gather.17.cloned.1.call-done = bf16[1152,1728]{1,0:T(8,128)(2,1)} async-done(((bf16[72,1728]{1,0:T(8,128)(2,1)}), bf16[1152,1728]{1,0:T(8,128)(2,1)}) %all-gather.17.cloned.1.call-update) | async-done | bytes 3981328 | tf_op jit(solution)/shard_map/all_gather | solution.py:67
  75.8 8.9 all-reduce.21
  85.8 82.3 %all-gather.19.cloned.1.call-done = bf16[1152,3456]{0,1:T(8,128)(2,1)} async-done(((bf16[1152,1728]{0,1:T(8,128)(2,1)}), bf16[1152,3456]{0,1:T(8,128)(2,1)}) %all-gather.19.cloned.1.call-update) | async-done | bytes 7962640 | tf_op jit(solution)/shard_map/all_gather | solution.py:73
  188.1 21.2 %all-gather.21.cloned.1.call-done = bf16[1152,576]{1,0:T(8,128)(2,1)} async-done(((bf16[72,576]{1,0:T(8,128)(2,1)}), bf16[1152,576]{1,0:T(8,128)(2,1)}) %all-gather.21.cloned.1.call-update) | async-done | bytes 1327120 | tf_op jit(solution)/shard_map/all_gather | solution.py:68
  211.9 53.1 %all-gather.25.cloned.1.call-done = bf16[1152,2152]{1,0:T(8,128)(2,1)} async-done(((bf16[72,2152]{1,0:T(8,128)(2,1)}), bf16[1152,2152]{1,0:T(8,128)(2,1)}) %all-gather.25.cloned.1.call-update) | async-done | bytes 4958224 | tf_op jit(solution)/shard_map/all_gather | solution.py:69
  265.0 8.5 copy.148
  277.5 32.7 %all-reduce.19 = (bf16[1024]{0:T(1024)(128)(2,1)S(1)}, bf16[1024]{0:T(1024)(128)(2,1)S(1)}, bf16[1024]{0:T(1024)(128)(2,1)S(1)}, bf16[1024]{0:T(1024)(128)(2,1)S(1)}) all-reduce(bf16[1024]{0:T(1024)(128)(2,1)S(1)} %dynamic-update-slice.10, bf16[1024]{0:T(1024)(128)(2,1)S(1)} %dynamic-update-slice.12, ...), channel_id=1, replica_groups=mesh['dev'=2,'sa'=16] {'sa'}, use_global_device_ids=true, to_apply=%add.10 | all-reduce | flops 4096 | bytes 16384
  310.8 10.2 all-gather.29.cloned.1.call-done
  321.0 8.4 copy.149
  332.0 44.0 %all-gather.35.cloned.1.call-done = bf16[1024,2304]{1,0:T(8,128)(2,1)} async-done(((bf16[64,2304]{1,0:T(8,128)(2,1)}), bf16[1024,2304]{1,0:T(8,128)(2,1)}) %all-gather.35.cloned.1.call-update) | async-done | bytes 4718608 | tf_op jit(solution)/shard_map/all_gather | solution.py:116
  382.7 48.1 %all-gather.37.cloned.1.call-done = bf16[1024,2304]{1,0:T(8,128)(2,1)} async-done(((bf16[64,2304]{1,0:T(8,128)(2,1)}), bf16[1024,2304]{1,0:T(8,128)(2,1)}) %all-gather.37.cloned.1.call-update) | async-done | bytes 4718608 | tf_op jit(solution)/shard_map/all_gather | solution.py:116
  438.5 47.1 %all-gather.39.cloned.1.call-done = bf16[1024,2304]{1,0:T(8,128)(2,1)} async-done(((bf16[64,2304]{1,0:T(8,128)(2,1)}), bf16[1024,2304]{1,0:T(8,128)(2,1)}) %all-gather.39.cloned.1.call-update) | async-done | bytes 4718608 | tf_op jit(solution)/shard_map/all_gather | solution.py:116
  543.8 106.0 %all-gather.27.cloned.1.call-done = bf16[1152,4304]{0,1:T(8,128)(2,1)} async-done(((bf16[1152,2152]{0,1:T(8,128)(2,1)}), bf16[1152,4304]{0,1:T(8,128)(2,1)}) %all-gather.27.cloned.1.call-update) | async-done | bytes 9916432 | tf_op jit(solution)/shard_map/all_gather | solution.py:75
  649.9 16.5 convolution_add_fusion.14
  666.4 108.3 %all-gather.31.cloned.1.call-done = bf16[1152,4304]{0,1:T(8,128)(2,1)} async-done(((bf16[1152,2152]{0,1:T(8,128)(2,1)}), bf16[1152,4304]{0,1:T(8,128)(2,1)}) %all-gather.31.cloned.1.call-update) | async-done | bytes 9916432 | tf_op jit(solution)/shard_map/all_gather | solution.py:76
  829.9 21.4 %copy.189 = bf16[1,1024,2304]{2,0,1:T(2,128)(2,1)} copy(bf16[1,1024,2304]{1,2,0:T(8,128)(2,1)} %pad_maximum_fusion.1) | data formatting | bytes 9437184
  871.4 21.5 %copy.193 = bf16[1,1024,2304]{2,0,1:T(2,128)(2,1)} copy(bf16[1,1024,2304]{1,2,0:T(8,128)(2,1)} %pad_maximum_fusion.3) | data formatting | bytes 9437184
  912.9 21.5 %copy.191 = bf16[1,1024,2304]{2,0,1:T(2,128)(2,1)} copy(bf16[1,1024,2304]{1,2,0:T(8,128)(2,1)} %pad_maximum_fusion.2) | data formatting | bytes 9437184
  963.3 49.4 %reduce-scatter.66.cloned.1.call-done = bf16[64,2304]{1,0:T(8,128)(2,1)} async-done(((bf16[1024,2304]{1,0:T(8,128)(2,1)}), bf16[64,2304]{1,0:T(8,128)(2,1)}) %reduce-scatter.66.cloned.1.call-update) | async-done | bytes 294928
  1016.8 74.2 %reduce-scatter.64.cloned.1.call-done = bf16[64,2304]{1,0:T(8,128)(2,1)} async-done(((bf16[1024,2304]{1,0:T(8,128)(2,1)}), bf16[64,2304]{1,0:T(8,128)(2,1)}) %reduce-scatter.64.cloned.1.call-update) | async-done | bytes 294928
  1115.5 49.6 %all-gather.33.cloned.1.call-done = bf16[1024,2304]{1,0:T(8,128)(2,1)} async-done(((bf16[64,2304]{1,0:T(8,128)(2,1)}), bf16[1024,2304]{1,0:T(8,128)(2,1)}) %all-gather.33.cloned.1.call-update) | async-done | bytes 4718608 | tf_op jit(solution)/shard_map/all_gather | solution.py:116
  1225.3 21.5 %copy.187 = bf16[1,1024,2304]{2,0,1:T(2,128)(2,1)} copy(bf16[1,1024,2304]{1,2,0:T(8,128)(2,1)} %pad_maximum_fusion) | data formatting | bytes 9437184
  1255.4 8.5 fusion.245
  1264.0 12.9 convolution_add_fusion.5
  1277.0 13.4 convolution_add_fusion.4
  1290.3 13.4 fusion
  1305.4 8.4 fusion.201
  1313.9 12.6 convolution_add_fusion.2
  1328.8 12.8 convolution_add_fusion.1
  1343.4 14.0 fusion.2
  1357.5 14.1 copy.201
  1381.9 11.2 fusion.156
  1393.1 8.7 convolution_add_fusion.8
  1401.9 8.2 convolution_add_fusion.7
  1410.1 11.2 fusion.3
  1433.4 9.1 all-reduce.20
  1470.5 18.1 reduce-scatter.58.cloned.1.call-done
  1503.6 12.8 reduce-scatter.78.cloned.1.call-done
  1518.0 12.8 reduce-scatter.80.cloned.1.call-done
  1532.4 12.8 reduce-scatter.70.cloned.1.call-done
  1546.9 119.3 %reduce-scatter.72.cloned.1.call-done = bf16[72,4304]{1,0:T(8,128)(2,1)} async-done(((bf16[1152,4304]{1,0:T(8,128)(2,1)}), bf16[72,4304]{1,0:T(8,128)(2,1)}) %reduce-scatter.72.cloned.1.call-update) | async-done | bytes 619792
  1674.3 96.4 %reduce-scatter.90.cloned.1.call-done = bf16[72,3456]{1,0:T(8,128)(2,1)} async-done(((bf16[1152,3456]{1,0:T(8,128)(2,1)}), bf16[72,3456]{1,0:T(8,128)(2,1)}) %reduce-scatter.90.cloned.1.call-update) | async-done | bytes 497680
  1775.0 10.2 reduce-scatter.74.cloned.1.call-done
  1786.3 13.7 reduce-scatter.76.cloned.1.call-done
  1801.0 13.3 reduce-scatter.84.cloned.1.call-done
  1815.3 13.3 reduce-scatter.82.cloned.1.call-done
  1829.7 63.4 %all-reduce.18 = (f32[1,576]{1,0:T(1,128)}, f32[1,576]{1,0:T(1,128)}, f32[1,576]{1,0:T(1,128)}, f32[1,576]{1,0:T(1,128)}, f32[1,576]{1,0:T(1,128)}, /*index=5*/f...) all-reduce(bf16[1,576]{1,0:T(2,128)(2,1)S(1)} %copy.204, ...), channel_id=1, replica_groups=mesh['dev'=2,'sa'=16] {'sa'}, use_global_device_ids=true, to_apply=%region_61.62 | all-reduce | flops 6760 | bytes 44864 | tf_op jit(solution)/shard_map/psum | solution.py:341
  1897.2 9.2 reduce-scatter.68.cloned.1.call-done
  (836 shorter events, 431.1 us)
Async XLA Ops:
  7.2 56.1 %all-gather.17.cloned.1.call-start = ((), (), s32[]{:S(2)}) async-start(), calls=%async_computation.19 | async-start | bytes 4386816 | tf_op jit(solution)/shard_map/all_gather | solution.py:67
  7.9 160.2 %all-gather.19.cloned.1.call-start = ((), (), s32[]{:S(2)}) async-start(), calls=%async_computation.20 | async-start | bytes 11943936 | tf_op jit(solution)/shard_map/all_gather | solution.py:73
  69.9 139.4 %all-gather.21.cloned.1.call-start = ((), (), s32[]{:S(2)}) async-start(), calls=%async_computation.21 | async-start | bytes 1566720 | tf_op jit(solution)/shard_map/all_gather | solution.py:68
  70.6 194.4 %all-gather.25.cloned.1.call-start = ((), (), s32[]{:S(2)}) async-start(), calls=%async_computation.23 | async-start | bytes 5326848 | tf_op jit(solution)/shard_map/all_gather | solution.py:69
  71.2 249.9 %all-gather.29.cloned.1.call-start = ((), (), s32[]{:S(2)}) async-start(), calls=%async_computation.25 | async-start | bytes 5326848 | tf_op jit(solution)/shard_map/all_gather | solution.py:70
  71.8 304.2 %all-gather.35.cloned.1.call-start = ((), (), s32[]{:S(2)}) async-start(), calls=%async_computation.29 | async-start | bytes 5013504 | tf_op jit(solution)/shard_map/all_gather | solution.py:116
  84.7 96.7 %copy-start.85 = (f32[1152]{0:T(1024)}, f32[1152]{0:T(1024)S(1)}, u32[]{:S(2)}) copy-start(f32[1152]{0:T(1024)S(1)} %mul.941) | copy-start | bytes 13828
  174.7 256.1 %all-gather.37.cloned.1.call-start = ((), (), s32[]{:S(2)}) async-start(), calls=%async_computation.30 | async-start | bytes 5013504 | tf_op jit(solution)/shard_map/all_gather | solution.py:116
  181.4 304.3 %all-gather.39.cloned.1.call-start = ((), (), s32[]{:S(2)}) async-start(), calls=%async_computation.31 | async-start | bytes 5013504 | tf_op jit(solution)/shard_map/all_gather | solution.py:116
  188.0 344.5 %all-gather.23.cloned.1.call-start = ((), (), s32[]{:S(2)}) async-start(), calls=%async_computation.22 | async-start | bytes 3981312 | tf_op jit(solution)/shard_map/all_gather | solution.py:74
  211.9 438.0 %all-gather.27.cloned.1.call-start = ((), (), s32[]{:S(2)}) async-start(), calls=%async_computation.24 | async-start | bytes 14874624 | tf_op jit(solution)/shard_map/all_gather | solution.py:75
  273.6 501.2 %all-gather.31.cloned.1.call-start = ((), (), s32[]{:S(2)}) async-start(), calls=%async_computation.26 | async-start | bytes 14874624 | tf_op jit(solution)/shard_map/all_gather | solution.py:76
  329.5 629.6 %reduce-scatter.62.cloned.1.call-start = ((), (), s32[]{:S(2)}) async-start(), calls=%async_computation.33 | async-start | bytes 5013504
  331.5 194.5 %copy-start.78 = (bf16[64,16,72]{2,1,0:T(8,128)(2,1)}, bf16[64,16,72]{2,1,0:T(8,128)(2,1)S(1)}, u32[]{:S(2)}) copy-start(bf16[64,16,72]{2,1,0:T(8,128)(2,1)S(1)} %reshape.1191) | copy-start | bytes 442372
  332.0 185.9 %copy-start.80 = (bf16[64,16,72]{2,1,0:T(8,128)(2,1)}, bf16[64,16,72]{2,1,0:T(8,128)(2,1)S(1)}, u32[]{:S(2)}) copy-start(bf16[64,16,72]{2,1,0:T(8,128)(2,1)S(1)} %reshape.1197) | copy-start | bytes 442372
  535.9 277.8 %copy-start.19 = (f32[64,1152]{1,0:T(8,128)}, f32[64,1152]{1,0:T(8,128)S(1)}, u32[]{:S(2)}) copy-start(f32[64,1152]{1,0:T(8,128)S(1)} %get-tuple-element.209) | copy-start | bytes 884740
  858.0 154.7 %reduce-scatter.66.cloned.1.call-start = ((), (), s32[]{:S(2)}) async-start(), calls=%async_computation.35 | async-start | bytes 5013504
  899.5 191.5 %reduce-scatter.64.cloned.1.call-start = ((), (), s32[]{:S(2)}) async-start(), calls=%async_computation.34 | async-start | bytes 5013504
  941.0 224.0 %all-gather.33.cloned.1.call-start = ((), (), s32[]{:S(2)}) async-start(), calls=%async_computation.28 | async-start | bytes 5013504 | tf_op jit(solution)/shard_map/all_gather | solution.py:116
  947.3 153.0 %copy-start.48 = (bf16[1,64,16,72]{1,3,2,0:T(8,128)(2,1)}, bf16[1,64,16,72]{1,3,2,0:T(8,128)(2,1)S(1)}, u32[]{:S(2)}) copy-start(bf16[1,64,16,72]{1,3,2,0:T(8,128)(2,1)S(1)} %copy.185) | copy-start | bytes 442372
  1112.4 229.1 %reduce-scatter.92.cloned.1.call-start = ((), (), s32[]{:S(2)}) async-start(), calls=%async_computation.49 | async-start | bytes 2820096
  1213.5 164.1 %reduce-scatter.60.cloned.1.call-start = ((), (), s32[]{:S(2)}) async-start(), calls=%async_computation.32 | async-start | bytes 5013504
  1253.6 169.4 %reduce-scatter.88.cloned.1.call-start = ((), (), s32[]{:S(2)}) async-start(), calls=%async_computation.46 | async-start | bytes 442368
  1255.3 233.4 %reduce-scatter.58.cloned.1.call-start = ((), (), s32[]{:S(2)}) async-start(), calls=%async_computation.27 | async-start | bytes 10653696 | tf_op jit(solution)/shard_map/reduce_scatter | solution.py:292
  1303.8 198.2 %reduce-scatter.86.cloned.1.call-start = ((), (), s32[]{:S(2)}) async-start(), calls=%async_computation.45 | async-start | bytes 442368
  1326.5 189.8 %reduce-scatter.78.cloned.1.call-start = ((), (), s32[]{:S(2)}) async-start(), calls=%async_computation.41 | async-start | bytes 442368
  1327.6 203.1 %reduce-scatter.80.cloned.1.call-start = ((), (), s32[]{:S(2)}) async-start(), calls=%async_computation.42 | async-start | bytes 442368
  1328.7 216.5 %reduce-scatter.70.cloned.1.call-start = ((), (), s32[]{:S(2)}) async-start(), calls=%async_computation.37 | async-start | bytes 442368
  1343.4 322.8 %reduce-scatter.72.cloned.1.call-start = ((), (), s32[]{:S(2)}) async-start(), calls=%async_computation.38 | async-start | bytes 10653696
  1371.6 399.1 %reduce-scatter.90.cloned.1.call-start = ((), (), s32[]{:S(2)}) async-start(), calls=%async_computation.48 | async-start | bytes 8460288
  1421.4 363.8 %reduce-scatter.74.cloned.1.call-start = ((), (), s32[]{:S(2)}) async-start(), calls=%async_computation.39 | async-start | bytes 442368
  1461.1 338.9 %reduce-scatter.76.cloned.1.call-start = ((), (), s32[]{:S(2)}) async-start(), calls=%async_computation.40 | async-start | bytes 442368
  1461.7 352.6 %reduce-scatter.84.cloned.1.call-start = ((), (), s32[]{:S(2)}) async-start(), calls=%async_computation.44 | async-start | bytes 442368
  1462.8 365.8 %reduce-scatter.82.cloned.1.call-start = ((), (), s32[]{:S(2)}) async-start(), calls=%async_computation.43 | async-start | bytes 442368
  1463.8 429.3 %all-reduce.24.cloned.1.call-start = ((), (), s32[]{:S(2)}) async-start(), calls=%async_computation.47 | async-start | bytes 1253376
  1488.7 406.3 %reduce-scatter.94.cloned.1.call-start = ((), (), s32[]{:S(2)}) async-start(), calls=%async_computation.50 | async-start | bytes 1652736
  1494.6 177.9 %copy-start.47 = (bf16[4,64,1152]{2,1,0:T(8,128)(2,1)S(1)}, bf16[4,64,1152]{2,1,0:T(8,128)(2,1)}, u32[]{:S(2)}) copy-start(bf16[4,64,1152]{2,1,0:T(8,128)(2,1)} %param.18) | copy-start | bytes 1769476
  1494.6 177.9 %copy-start.53 = (f32[64,1152]{1,0:T(8,128)S(1)}, f32[64,1152]{1,0:T(8,128)}, u32[]{:S(2)}) copy-start(f32[64,1152]{1,0:T(8,128)} %copy-done.51) | copy-start | bytes 884740
  1494.7 177.9 %copy-start.57 = (f32[64,1152]{1,0:T(8,128)S(1)}, f32[64,1152]{1,0:T(8,128)}, u32[]{:S(2)}) copy-start(f32[64,1152]{1,0:T(8,128)} %copy-done.55) | copy-start | bytes 884740
  1494.7 177.9 %copy-start.67 = (f32[64,1152]{1,0:T(8,128)S(1)}, f32[64,1152]{1,0:T(8,128)}, u32[]{:S(2)}) copy-start(f32[64,1152]{1,0:T(8,128)} %copy-done.66) | copy-start | bytes 884740
  1494.7 177.9 %copy-start.69 = (f32[64,1152]{1,0:T(8,128)S(1)}, f32[64,1152]{1,0:T(8,128)}, u32[]{:S(2)}) copy-start(f32[64,1152]{1,0:T(8,128)} %copy-done.68) | copy-start | bytes 884740
  1668.5 104.5 %copy-start.65 = (f32[64,1152]{1,0:T(8,128)S(1)}, f32[64,1152]{1,0:T(8,128)}, u32[]{:S(2)}) copy-start(f32[64,1152]{1,0:T(8,128)} %copy-done.64) | copy-start | bytes 884740
  1668.5 104.5 %copy-start.71 = (f32[64,1152]{1,0:T(8,128)S(1)}, f32[64,1152]{1,0:T(8,128)}, u32[]{:S(2)}) copy-start(f32[64,1152]{1,0:T(8,128)} %copy-done.70) | copy-start | bytes 884740
  1668.5 104.5 %copy-start.73 = (f32[64,1152]{1,0:T(8,128)S(1)}, f32[64,1152]{1,0:T(8,128)}, u32[]{:S(2)}) copy-start(f32[64,1152]{1,0:T(8,128)} %copy-done.72) | copy-start | bytes 884740
  1668.5 104.5 %copy-start.75 = (f32[64,1152]{1,0:T(8,128)S(1)}, f32[64,1152]{1,0:T(8,128)}, u32[]{:S(2)}) copy-start(f32[64,1152]{1,0:T(8,128)} %get-tuple-element.217) | copy-start | bytes 884740
  1668.5 237.8 %reduce-scatter.68.cloned.1.call-start = ((), (), s32[]{:S(2)}) async-start(), calls=%async_computation.36 | async-start | bytes 1327104
  1674.3 99.8 %copy-start.105 = (bf16[1,64,1152]{2,1,0:T(8,128)(2,1)S(1)}, bf16[1,64,1152]{2,1,0:T(8,128)(2,1)}, u32[]{:S(2)}) copy-start(bf16[1,64,1152]{2,1,0:T(8,128)(2,1)} %get-tuple-element.168) | copy-start | bytes 442372
  1674.3 99.8 %copy-start.106 = (bf16[1,64,1152]{2,1,0:T(8,128)(2,1)S(1)}, bf16[1,64,1152]{2,1,0:T(8,128)(2,1)}, u32[]{:S(2)}) copy-start(bf16[1,64,1152]{2,1,0:T(8,128)(2,1)} %get-tuple-element.169) | copy-start | bytes 442372
  (231 other events, 2464.1 us)
Sparse Core Ops, SparseCore 0:
  10.3 52.9 all-gather.16
  70.0 98.0 all-gather.18
  170.3 38.9 all-gather.20
  211.3 53.7 all-gather.24
  267.0 53.9 all-gather.28
  323.8 52.1 all-gather.34
  378.8 51.9 all-gather.36
  433.6 51.9 all-gather.38
  487.2 37.9 all-gather.22
  526.5 123.3 all-gather.26
  651.5 123.2 all-gather.30
  858.1 75.5 reduce-scatter.61
  938.0 74.6 reduce-scatter.65
  1016.4 74.5 reduce-scatter.63
  1112.6 52.4 all-gather.32
  1213.6 62.4 reduce-scatter.91
  1279.8 74.4 reduce-scatter.59
  1356.4 11.0 reduce-scatter.87
  1372.2 116.4 reduce-scatter.57
  1490.8 11.0 reduce-scatter.85
  1504.3 12.0 reduce-scatter.77
  1518.7 12.0 reduce-scatter.79
  1533.1 12.0 reduce-scatter.69
  1549.8 116.4 reduce-scatter.71
  1670.8 99.8 reduce-scatter.89
  1773.4 11.8 reduce-scatter.73
  1787.9 12.0 reduce-scatter.75
  1802.2 12.0 reduce-scatter.83
  1816.5 12.0 reduce-scatter.81
  1830.8 30.8 all-reduce.23
  1863.9 21.4 reduce-scatter.93
  1887.8 18.5 reduce-scatter.67
where the time goes:
time: 1930 us; the launch traced here: 1920 us
  waiting for transfers between devices  1090 us (56%)
  matrix products  339 us (18%)
  local copies, waits for them, and re-layouts  299 us (15%)
  blocking collectives  114 us (6%)
  other arithmetic  49.7 us (3%)
  between operations  20.6 us (1%)
    unnamed x51, waiting for transfers between devices  446 us
    unnamed x562, local copies, waits for them, and re-layouts  197 us
    all_gather x4, waiting for transfers between devices, per_device(): lax.all_gather(key_value, 'sa', axis=1, tiled=True)  189 us
    dot_general x16, matrix products, mat_rows(): lax.dot_general(left, right, (((0,), (0,)), ((), ())), preferred_element_...  140 us
    all_gather x1, waiting for transfers between devices, per_device(): lax.all_gather(row_parts[3], 'dev', axis=1, tiled=True)  108 us
    all_gather x1, waiting for transfers between devices, per_device(): lax.all_gather(row_parts[2], 'dev', axis=1, tiled=True)  106 us
    all_gather x1, waiting for transfers between devices, per_device(): lax.all_gather(row_parts[0], 'dev', axis=1, tiled=True)  82.3 us
    psum x1, blocking collectives, per_device(): lax.psum((column_sums[4], column_sums[5], column_sums[6], column_sums[7],...  63.4 us
  transfers between devices with their start and end apart: 32, of which 25 were waited for; matrix products, arithmetic and copies ran while one was open for 27% of the time, Pallas kernels for 0%

commit v1 on v0

v1 whole, which is shorter than its diff:
```python
import functools

import jax
import jax.numpy as jnp
from jax import lax
from jax.experimental import pallas as pl
from jax.experimental.pallas import tpu as pltpu
from jax.sharding import Mesh
from jax.sharding import PartitionSpec as P

HEADS = 16
HEAD_DIM = 72
SCALE = HEAD_DIM ** (-0.5)
Q_BLOCK = 256
F32 = jnp.float32
BF16 = jnp.bfloat16


def dot(left, right):
    return jnp.dot(left, right, preferred_element_type=F32)


def dot_tn(left, right):
    return lax.dot_general(left, right, (((0,), (0,)), ((), ())), preferred_element_type=F32)


def dot_nt(left, right):
    return lax.dot_general(left, right, (((1,), (1,)), ((), ())), preferred_element_type=F32)


def attend_fwd_body(heads, qkv_ref, bias_ref, out_ref, lse_ref):
    width = heads * HEAD_DIM
    begin = pl.program_id(1) * Q_BLOCK
    bias = bias_ref[0]
    lane = lax.broadcasted_iota(jnp.int32, (Q_BLOCK, 128), 1)
    stats = jnp.zeros((Q_BLOCK, 128), F32)
    for head in range(heads):
        low = head * HEAD_DIM
        query = qkv_ref[0, pl.ds(begin, Q_BLOCK), low : low + HEAD_DIM]
        keys = qkv_ref[0, :, width + low : width + low + HEAD_DIM]
        values = qkv_ref[0, :, 2 * width + low : 2 * width + low + HEAD_DIM]
        scores = dot_nt(query, keys) * SCALE + bias
        peak = jnp.max(scores, axis=1, keepdims=True)
        expo = jnp.exp(scores - peak)
        total = jnp.sum(expo, axis=1, keepdims=True)
        mixed = dot(expo.astype(BF16), values) / total
        out_ref[0, :, low : low + HEAD_DIM] = mixed.astype(BF16)
        stats = jnp.where(lane == head, peak + jnp.log(total), stats)
    lse_ref[0] = jnp.transpose(stats)[:8]


def attend_bwd_body(heads, qkv_ref, bias_ref, lse_ref, grad_ref, out_ref, key_acc, value_acc):
    width = heads * HEAD_DIM
    step = pl.program_id(1)
    begin = step * Q_BLOCK
    bias = bias_ref[0]

    @pl.when(step == 0)
    def _():
        key_acc[...] = jnp.zeros_like(key_acc)
        value_acc[...] = jnp.zeros_like(value_acc)

    for head in range(heads):
        low = head * HEAD_DIM
        rows = pl.ds(begin, Q_BLOCK)
        query = qkv_ref[0, rows, low : low + HEAD_DIM]
        grad = grad_ref[0, :, low : low + HEAD_DIM]
        keys = qkv_ref[0, :, width + low : width + low + HEAD_DIM]
        values = qkv_ref[0, :, 2 * width + low : 2 * width + low + HEAD_DIM]
        scores = dot_nt(keys, query) * SCALE + bias
        probs = jnp.exp(scores - lse_ref[0, head : head + 1, :])
        value_acc[head] += dot(probs.astype(BF16), grad)
        grad_probs = dot_nt(values, grad)
        term = jnp.sum(probs * grad_probs, axis=0, keepdims=True)
        grad_scores = (probs * (grad_probs - term)).astype(BF16)
        key_acc[head] += dot(grad_scores, query)
        grad_query = dot_tn(grad_scores, keys) * SCALE
        out_ref[0, rows, low : low + HEAD_DIM] = grad_query.astype(BF16)

    @pl.when(step == pl.num_programs(1) - 1)
    def _():
        for head in range(heads):
            low = head * HEAD_DIM
            out_ref[0, :, width + low : width + low + HEAD_DIM] = (key_acc[head] * SCALE).astype(BF16)
            out_ref[0, :, 2 * width + low : 2 * width + low + HEAD_DIM] = value_acc[head].astype(BF16)


def attend_fwd(qkv, bias, heads):
    images, seq, wide = qkv.shape
    width = heads * HEAD_DIM
    steps = seq // Q_BLOCK
    work = images * heads * seq * seq
    return pl.pallas_call(
        functools.partial(attend_fwd_body, heads),
        name="attend_fwd",
        grid=(images, steps),
        in_specs=[
            pl.BlockSpec((1, seq, wide), lambda i, j: (i, 0, 0)),
            pl.BlockSpec((1, 1, seq), lambda i, j: (i, 0, 0)),
        ],
        out_specs=[
            pl.BlockSpec((1, Q_BLOCK, width), lambda i, j: (i, j, 0)),
            pl.BlockSpec((1, 8, Q_BLOCK), lambda i, j: (i, 0, j)),
        ],
        out_shape=[
            jax.ShapeDtypeStruct((images, seq, width), BF16),
            jax.ShapeDtypeStruct((images, 8, seq), F32),
        ],
        cost_estimate=pl.CostEstimate(
            flops=4 * work * 128, transcendentals=work, bytes_accessed=images * seq * wide * 3
        ),
        compiler_params=pltpu.CompilerParams(vmem_limit_bytes=40 << 20),
    )(qkv, bias)


def attend_bwd(qkv, bias, lse, grad, heads):
    images, seq, wide = qkv.shape
    width = heads * HEAD_DIM
    steps = seq // Q_BLOCK
    work = images * heads * seq * seq
    return pl.pallas_call(
        functools.partial(attend_bwd_body, heads),
        name="attend_bwd",
        grid=(images, steps),
        in_specs=[
            pl.BlockSpec((1, seq, wide), lambda i, j: (i, 0, 0)),
            pl.BlockSpec((1, seq, 1), lambda i, j: (i, 0, 0)),
            pl.BlockSpec((1, 8, Q_BLOCK), lambda i, j: (i, 0, j)),
            pl.BlockSpec((1, Q_BLOCK, width), lambda i, j: (i, j, 0)),
        ],
        out_specs=pl.BlockSpec((1, seq, wide), lambda i, j: (i, 0, 0)),
        out_shape=jax.ShapeDtypeStruct((images, seq, wide), BF16),
        scratch_shapes=[
            pltpu.VMEM((heads, seq, HEAD_DIM), F32),
            pltpu.VMEM((heads, seq, HEAD_DIM), F32),
        ],
        cost_estimate=pl.CostEstimate(
            flops=10 * work * 128, transcendentals=work, bytes_accessed=images * seq * wide * 5
        ),
        compiler_params=pltpu.CompilerParams(vmem_limit_bytes=48 << 20),
    )(qkv, bias, lse, grad)


class Native:
    def __init__(self, sizes, images, tokens):
        self.dev, self.zed, self.why = sizes
        self.images = images
        self.tokens = tokens
        self.team = self.dev * 2
        self.groups = self.zed * self.why
        self.each = images * self.dev // self.groups
        self.piece = tokens // self.dev
        self.rows = self.each * self.groups * self.piece

    def image_ids(self):
        group = lax.axis_index(("z", "y"))
        return group * self.each + jnp.arange(self.each)

    def positions(self):
        shape = (self.team, self.groups, self.piece)
        team = lax.broadcasted_iota(jnp.int32, shape, 0)
        group = lax.broadcasted_iota(jnp.int32, shape, 1)
        place = lax.broadcasted_iota(jnp.int32, shape, 2)
        owner = group * 2 + team % 2
        return (owner * self.tokens + (team // 2) * self.piece + place).reshape(-1)

    def tokens_in(self, values):
        wide = values.shape[-1]
        split = values.reshape(self.images, self.dev, self.piece, wide)
        split = lax.all_to_all(split, "dev", 1, 0, tiled=True)
        split = split.reshape(self.groups, self.each, self.piece, wide)
        split = lax.all_to_all(split, ("z", "y"), 0, 0, tiled=True)
        return split.transpose(1, 0, 2, 3).reshape(self.rows, wide)

    def tokens_out(self, values):
        wide = values.shape[-1]
        split = values.reshape(self.each, self.groups, self.piece, wide).transpose(1, 0, 2, 3)
        split = lax.all_to_all(split, ("z", "y"), 0, 0, tiled=True)
        split = split.reshape(self.dev * self.images, 1, self.piece, wide)
        split = lax.all_to_all(split, "dev", 0, 1, tiled=True)
        return split.reshape(self.images, self.tokens, wide)

    def rows_gather(self, values):
        wide = values.shape[-1]
        whole = lax.all_gather(values, ("dev", "core"), axis=0, tiled=True)
        whole = whole.reshape(self.team, self.each, -1, wide).transpose(1, 0, 2, 3)
        return whole.reshape(self.team * self.rows, wide)

    def rows_scatter(self, values):
        wide = values.shape[-1]
        split = values.astype(BF16).reshape(self.each, self.team, -1, wide).transpose(1, 0, 2, 3)
        split = split.reshape(self.team * self.rows, wide)
        return lax.psum_scatter(
            split, ("dev", "core"), scatter_dimension=0, tiled=True
        ).astype(F32)

    def own_rows(self, values):
        wide = values.shape[-1]
        me = lax.axis_index(("dev", "core"))
        split = values.reshape(self.each, self.team, -1, wide)
        return lax.dynamic_slice_in_dim(split, me, 1, 1).reshape(self.rows, wide)

    def columns_gather(self, values):
        return lax.all_gather(values, ("dev", "core"), axis=1, tiled=True)

    def heads_gather(self, values):
        return self.columns_gather(values)

    def heads_in(self, shard):
        whole = lax.all_gather(shard, "dev", axis=1, tiled=True)
        rows, wide = whole.shape
        split = whole.reshape(rows, 3, self.dev, wide // (3 * self.dev))
        split = lax.dynamic_slice_in_dim(split, lax.axis_index("dev"), 1, 2)
        return split.reshape(rows, 3, wide // (3 * self.dev))

    def heads_out(self, block):
        rows, _, wide = block.shape
        whole = lax.all_gather(block[:, :, None, :], "dev", axis=2, tiled=True)
        whole = whole.reshape(rows, self.dev, 3 * wide)
        return lax.dynamic_slice_in_dim(whole, lax.axis_index("dev"), 1, 1)[:, 0]


def joint(move):
    pairs = []
    for dev in range(2):
        for zed in range(4):
            for why in range(2):
                for core in range(2):
                    to = move(dev, zed, why, core)
                    source = ((dev * 4 + zed) * 2 + why) * 2 + core
                    pairs.append((source, ((to[0] * 4 + to[1]) * 2 + to[2]) * 2 + to[3]))
    return pairs


def send(values, move):
    return lax.ppermute(values, ("dev", "z", "y", "core"), joint(move))


def across(values):
    return send(values, lambda d, z, y, c: (1 - d, z, y, c))


def beside(values):
    return send(values, lambda d, z, y, c: (d, z, y, 1 - c))


class Paired(Native):
    def image_ids(self):
        return (lax.axis_index("y") * 4 + lax.axis_index("z")).reshape(1)

    def positions(self):
        shape = (4, 4, self.tokens)
        block = lax.broadcasted_iota(jnp.int32, shape, 0)
        turn = lax.broadcasted_iota(jnp.int32, shape, 1)
        place = lax.broadcasted_iota(jnp.int32, shape, 2)
        why = lax.axis_index("dev") ^ (block // 2)
        core = lax.axis_index("core") ^ (block % 2)
        zed = (lax.axis_index("z") - turn) % 4
        return (((zed * 2 + why) * 2 + core) * self.tokens + place).reshape(-1)

    def tokens_in(self, values):
        zed = lax.axis_index("z")
        pieces = []
        for turn in range(4):
            piece = lax.dynamic_slice_in_dim(values, (zed + turn) % 4, 1, 0)[0]
            pieces.append(send(piece, lambda d, z, y, c: (y, (z + turn) % 4, d, c)))
        return jnp.concatenate(pieces, axis=0)

    def tokens_out(self, values):
        zed = lax.axis_index("z")
        rows = self.tokens
        pieces = []
        for turn in range(4):
            piece = values[turn * rows : (turn + 1) * rows]
            pieces.append(send(piece, lambda d, z, y, c: (y, (z - turn) % 4, d, c)))
        stacked = jnp.stack(pieces, axis=0)
        order = (jnp.arange(4) - zed) % 4
        return sum(
            jnp.where((order == turn)[:, None, None], stacked[turn][None], 0) for turn in range(4)
        ).astype(values.dtype)

    def rows_gather(self, values):
        far = across(values)
        return jnp.concatenate([values, beside(values), far, beside(far)], axis=0)

    def rows_scatter(self, values):
        rows = self.rows
        near = jnp.concatenate([values[rows : 2 * rows], values[3 * rows :]], axis=0)
        came = beside(near.astype(BF16)).astype(F32)
        held = values[:rows] + came[:rows]
        away = values[2 * rows : 3 * rows] + came[rows:]
        return held + across(away.astype(BF16)).astype(F32)

    def own_rows(self, values):
        return values[: self.rows]

    def heads_gather(self, values):
        return self.columns_gather(values, True)

    def columns_gather(self, values, by_rows=False):
        far = across(values)
        pieces = [values, beside(values), far, beside(far)]
        if by_rows:
            rows = self.rows
            for step in range(1, 4):
                pieces[step] = jnp.concatenate(
                    [pieces[step][(k ^ step) * rows : ((k ^ step) + 1) * rows] for k in range(4)]
                )
        me = lax.axis_index(("dev", "core"))
        ordered = []
        for place in range(4):
            pick = place ^ me
            out = pieces[0]
            for other in range(1, 4):
                out = jnp.where(pick == other, pieces[other], out)
            ordered.append(out)
        return jnp.concatenate(ordered, axis=1)

    def heads_in(self, shard):
        half = shard.shape[1] // 3
        first = lax.axis_index("dev") == 0
        came = across(shard[:, half : 2 * half])
        low, high = shard[:, :half], shard[:, 2 * half :]
        query = jnp.where(first, low, came)
        keys = jnp.where(first, high, low)
        values = jnp.where(first, came, high)
        return jnp.stack([query, keys, values], axis=1)

    def heads_out(self, block):
        first = lax.axis_index("dev") == 0
        query, keys, values = block[:, 0], block[:, 1], block[:, 2]
        came = across(jnp.where(first, values, query))
        return jnp.concatenate(
            [jnp.where(first, query, keys), came, jnp.where(first, keys, values)], axis=1
        )


def core_in(shard):
    return lax.all_to_all(shard, "core", 1, 0, tiled=True)


def core_out(block):
    return lax.all_to_all(block, "core", 0, 1, tiled=True)


def centred(values):
    centre = values - jnp.mean(values, axis=-1, keepdims=True)
    spread = jnp.mean(centre * centre, axis=-1, keepdims=True)
    inverse = lax.rsqrt(spread + 1e-06)
    return centre * inverse, inverse


def norm_back(grad, unit, inverse, gain):
    scaled = grad * gain
    mean = jnp.mean(scaled, axis=-1, keepdims=True)
    along = jnp.mean(scaled * unit, axis=-1, keepdims=True)
    return (scaled - mean - unit * along) * inverse


def gelu_pair(hidden):
    root = 0.7978845608028654
    inner = jnp.tanh(root * (hidden + 0.044715 * hidden * hidden * hidden))
    half = 0.5 * (1.0 + inner)
    slope = half + 0.5 * hidden * (1.0 - inner * inner) * root * (
        1.0 + 3 * 0.044715 * hidden * hidden
    )
    return hidden * half, slope


def per_device(
    sizes,
    patches,
    patch_mask,
    cotangent,
    w_qkv,
    w_out,
    w_up,
    w_down,
    *vectors,
):
    images, tokens, width = patches.shape
    paired = sizes == (2, 4, 2) and images == 4 and Paired is not Native
    route = (Paired if paired else Native)(sizes, images, tokens)
    dev_count = sizes[0]
    team = route.team
    everyone = ("dev", "z", "y", "core")
    plane = ("z", "y")
    dev = lax.axis_index("dev")
    me = lax.axis_index(("dev", "core"))
    head_count = HEADS // team
    block = head_count * HEAD_DIM
    hidden = w_up.shape[1] // 2

    counts = jnp.zeros((dev_count, images), F32)
    counts = lax.dynamic_update_slice(
        counts, jnp.sum(patch_mask, axis=1).astype(F32)[None], (dev, 0)
    )
    lengths = lax.psum(counts.reshape(1, -1), everyone)[0]

    packed = jnp.concatenate(vectors, axis=1)
    if paired:
        other = across(packed)
        lower = jnp.where(dev == 0, packed, other)[0].astype(F32)
        upper = jnp.where(dev == 0, other, packed)[0].astype(F32)
        halves = jnp.stack([lower, upper])
    else:
        halves = lax.all_gather(packed, "dev", axis=0, tiled=True).astype(F32)
    full = []
    spot = 0
    for item in vectors:
        full.append(halves[:, spot : spot + item.shape[1]].reshape(-1))
        spot += item.shape[1]
    gain_one, shift_one, gain_two, shift_two = full[:4]
    bias_query, bias_value, bias_out, bias_up, bias_down = full[4:]

    own_in = route.tokens_in(patches)
    rows_in = route.rows_gather(own_in)

    qkv_shard = route.heads_in(w_qkv)
    parts = qkv_shard.shape[2] // 2
    qkv_shard = core_in(
        qkv_shard.reshape(-1, 3, 2, parts).transpose(0, 2, 1, 3).reshape(-1, 6 * parts)
    )
    own_qkv = lax.all_gather(qkv_shard, plane, axis=0, tiled=True)
    shards = [core_in(w_out), core_in(w_up), core_in(w_down)]
    rest = lax.all_gather(jnp.concatenate(shards, axis=1), plane, axis=0, tiled=True)
    column_out = rest[:, :block]
    own_up = rest[:, block : block + hidden]
    own_down = rest[:, block + hidden :]
    full_out = route.columns_gather(column_out)
    rows_out = lax.dynamic_slice_in_dim(full_out, me * block, block, 0)

    own_grad = route.tokens_in(cotangent)
    rows_grad = route.rows_gather(own_grad)

    inputs = rows_in.astype(F32)
    unit_one, inverse_one = centred(inputs)
    normed_one = (unit_one * gain_one + shift_one).astype(BF16)
    qkv_bias = jnp.concatenate(
        [
            lax.dynamic_slice_in_dim(bias_query, me * block, block),
            jnp.zeros((block,), F32),
            lax.dynamic_slice_in_dim(bias_value, me * block, block),
        ]
    )
    projected = (dot(normed_one, own_qkv) + qkv_bias).astype(BF16)
    seq = projected.shape[0] // route.each
    projected = projected.reshape(route.each, seq, 3 * block)
    own_lengths = lengths[route.image_ids()]
    valid = route.positions()[None, :].astype(F32) < own_lengths[:, None]
    mask_bias = jnp.where(valid, 0.0, -1e30).astype(F32)
    attended, lse = attend_fwd(projected, mask_bias[:, None, :], head_count)
    all_attended = route.heads_gather(attended.reshape(-1, block))
    middle = inputs + dot(all_attended, full_out) + bias_out
    unit_two, inverse_two = centred(middle)
    normed_two = (unit_two * gain_two + shift_two).astype(BF16)
    up_bias = lax.dynamic_slice_in_dim(bias_up, me * hidden, hidden)
    hidden_pre = dot(normed_two, own_up) + up_bias
    active, slope = gelu_pair(hidden_pre)
    active = active.astype(BF16)

    grad_active = dot(rows_grad, own_down)
    grad_hidden = (grad_active * slope).astype(BF16)
    grad_normed_two = route.rows_scatter(dot_nt(grad_hidden, own_up))
    own_unit_two = route.own_rows(unit_two)
    own_inverse_two = route.own_rows(inverse_two)
    grad_middle = own_grad.astype(F32) + norm_back(
        grad_normed_two, own_unit_two, own_inverse_two, gain_two
    )
    own_branch = grad_middle.astype(BF16)
    grad_branch = route.rows_gather(own_branch)

    mlp_part = route.rows_scatter(dot_nt(active, own_down))
    result = (route.own_rows(middle) + mlp_part + bias_down).astype(BF16)
    result = route.tokens_out(result)

    grad_down = dot_tn(rows_grad, active)
    grad_up = dot_tn(normed_two, grad_hidden)

    grad_attended = dot_nt(grad_branch, rows_out).astype(BF16)
    grad_projected = attend_bwd(
        projected,
        mask_bias[:, :, None],
        lse,
        grad_attended.reshape(route.each, seq, block),
        head_count,
    ).reshape(-1, 3 * block)
    grad_normed_one = route.rows_scatter(dot_nt(grad_projected, own_qkv))
    own_unit_one = route.own_rows(unit_one)
    grad_inputs = grad_middle + norm_back(
        grad_normed_one, own_unit_one, route.own_rows(inverse_one), gain_one
    )
    grad_patches = route.tokens_out(grad_inputs.astype(BF16))

    my_branch = lax.dynamic_slice_in_dim(grad_branch, me * block, block, 1)
    grad_out = dot_tn(all_attended, my_branch)
    grad_qkv = dot_tn(normed_one, grad_projected)

    def summed(values):
        return lax.psum_scatter(values.astype(BF16), plane, scatter_dimension=0, tiled=True)

    sum_mlp = summed(jnp.concatenate([grad_down, grad_up], axis=1))
    sum_attn = summed(jnp.concatenate([grad_out, grad_qkv], axis=1))
    out_down = core_out(sum_mlp[:, :hidden]).astype(F32)
    out_up = core_out(sum_mlp[:, hidden:]).astype(F32)
    out_out = core_out(sum_attn[:, :block]).astype(F32)
    piece = core_out(sum_attn[:, block:])
    piece = piece.reshape(-1, 2, 3, block).transpose(0, 2, 1, 3).reshape(-1, 3, 2 * block)
    out_qkv = route.heads_out(piece).astype(F32)

    def spread(values, size):
        return lax.dynamic_update_slice(
            jnp.zeros((size,), F32), values, (me * values.shape[0],)
        )

    proj_sums = jnp.sum(grad_projected.astype(F32), axis=0)
    sums = [
        jnp.sum(grad_normed_one * own_unit_one, axis=0),
        jnp.sum(grad_normed_one, axis=0),
        jnp.sum(grad_normed_two * own_unit_two, axis=0),
        jnp.sum(grad_normed_two, axis=0),
        spread(proj_sums[:block], width),
        spread(proj_sums[2 * block :], width),
        jnp.sum(own_branch.astype(F32), axis=0),
        spread(jnp.sum(grad_hidden.astype(F32), axis=0), hidden * team),
        jnp.sum(cotangent.astype(F32), axis=(0, 1)),
    ]
    flat = lax.psum(jnp.concatenate(sums)[None], everyone)
    out_vectors = []
    spot = 0
    for item in sums:
        size = item.shape[0]
        half = size // dev_count
        out_vectors.append(lax.dynamic_slice(flat, (0, spot + dev * half), (1, half)))
        spot += size
    return (result, grad_patches, out_qkv, out_out, out_up, out_down, *out_vectors)


def solution(mesh):
    dev_count, sa_count = mesh.devices.shape

    def whole(*args):
        zed = args[0].shape[0] // dev_count
        why = sa_count // (2 * zed)
        sizes = (dev_count, zed, why)
        inner = Mesh(mesh.devices.reshape(dev_count, zed, why, 2), ("dev", "z", "y", "core"))
        rows = ("z", "y", "core")
        token = P("dev", rows, None)
        weight = P(rows, "dev")
        vector = P(None, "dev")
        return jax.shard_map(
            functools.partial(per_device, sizes),
            mesh=inner,
            in_specs=(token, P("dev", rows), token) + (weight,) * 4 + (vector,) * 9,
            out_specs=(token, token) + (weight,) * 4 + (vector,) * 9,
            check_vma=False,
        )(*args)

    return whole
```

time: 1930 us -> 567 us (0.29)
  the two profiles are of different devices: /device:TPU:0 before, /device:TPU:11 now
where the time goes in v1:
time: 567 us; the launch traced here: 560 us
  waiting for transfers between devices  135 us (24%)
  blocking collectives  102 us (18%)
  local copies, waits for them, and re-layouts  101 us (18%)
  starting transfers between devices  64.3 us (11%)
  matrix products  59.8 us (11%)
  other arithmetic  49.1 us (9%)
  Pallas kernels  33.3 us (6%)
  between operations  15.4 us (3%)
    ppermute x40, waiting for transfers between devices, send(): return lax.ppermute(values, ('dev', 'z', 'y', 'core'), joint(move))  134 us
    ppermute x40, starting transfers between devices, send(): return lax.ppermute(values, ('dev', 'z', 'y', 'core'), joint(move))  48.1 us
    unnamed x144, local copies, waits for them, and re-layouts  44 us
    psum x1, blocking collectives, per_device(): flat = lax.psum(jnp.concatenate(sums)[None], everyone)  42.8 us
    psum x1, blocking collectives, per_device(): lengths = lax.psum(counts.reshape(1, -1), everyone)[0]  40.5 us
    dot_general x4, matrix products, dot_nt(): lax.dot_general(left, right, (((1,), (1,)), ((), ())), preferred_element_...  22.1 us
    dot_general x4, matrix products, dot(): return jnp.dot(left, right, preferred_element_type=F32)  21.7 us
    pallas_call x1, Pallas kernels, attend_bwd(): pl.pallas_call(functools.partial(attend_bwd_body, heads), name='attend_bw...  19.8 us
  transfers between devices with their start and end apart: 48, of which 17 were waited for; matrix products, arithmetic and copies ran while one was open for 25% of the time, Pallas kernels for 2%

profile of v1, /device:TPU:11, one launch (start us, length us, event | category | flops | bytes accessed | tf_op | source)
XLA Modules:
  0.0 559.8 jit_solution(16854311164522353369)
XLA Ops:
  8.6 3.1 collective-permute-done.8
  14.8 6.1 %all_to_all.131 = bf16[72,2,864]{2,0,1:T(8,128)(2,1)} all-to-all(bf16[72,2,864]{2,0,1:T(8,128)(2,1)S(1)} %all_to_all.98), channel_id=1, replica_groups=mesh['dev'=2,'z'=4,'y'=2,'core'=2] {'core'}, dimensions={1} | all-to-all | bytes 497664 | tf_op jit(solution)/shard_map/all_to_all | solution.py:339
  22.3 4.0 all-to-all-start.1
  27.4 4.0 all_to_all.132
  31.4 4.1 all_to_all.133
  40.4 4.1 collective-permute-start
  44.7 4.0 collective-permute-start.2
  48.7 40.5 %psum.14 = f32[8]{0:T(128)S(1)} all-reduce(f32[8]{0:T(128)S(1)} %squeeze.36), channel_id=1, replica_groups=mesh['dev'=2,'z'=4,'y'=2,'core'=2] {'dev','z','y','core'}, use_global_device_ids=true, to_apply=%region_3.4 | all-reduce | flops 8 | bytes 64 | tf_op jit(solution)/shard_map/psum | solution.py:398
  99.8 3.1 collective-permute-start.21
  103.6 5.5 collective-permute-done.21
  109.8 12.8 %collective-permute-done.22 = bf16[64,1152]{1,0:T(8,128)(2,1)S(1)} collective-permute-done((bf16[64,1152]{1,0:T(8,128)(2,1)S(1)}, bf16[64,1152]{1,0:T(8,128)(2,1)S(1)}, u32[]{:S(2)}, u32[]{:S(2)}) %collective-permute-start.22) | collective-permute-done | bytes 147488 | tf_op jit(solution)/shard_map/ppermute | solution.py:236
  127.6 13.4 %collective-permute-done.26 = bf16[256,1152]{1,0:T(8,128)(2,1)} collective-permute-done((bf16[256,1152]{1,0:T(8,128)(2,1)}, bf16[256,1152]{1,0:T(8,128)(2,1)}, u32[]{:S(2)}, u32[]{:S(2)}) %collective-permute-start.26) | collective-permute-done | bytes 589856 | tf_op jit(solution)/shard_map/ppermute | solution.py:236
  144.4 4.5 fusion.16.qkv_ref
  148.9 13.5 %attend_fwd.1 = (bf16[1,1024,288]{2,1,0:T(8,128)(2,1)S(1)}, f32[1,8,1024]{2,1,0:T(8,128)S(1)}) custom-call(bf16[1,1024,864]{2,1,0:T(8,128)(2,1)S(1)} %fusion.16.qkv_ref, f32[1,1,1024]{2,1,0:T(1,128)S(1)} %compare_select_fusion.2.bias_ref), custom_call_target="tpu_custom_call" | custom-call | flops 2147483648 | bytes 2654208 | tf_op jit(solution)/shard_map/attend_fwd/pallas_call | solution.py:93
  170.1 8.7 %collective-permute-done.9 = bf16[1024,288]{0,1:T(8,128)(2,1)} collective-permute-done((bf16[1024,288]{0,1:T(8,128)(2,1)}, bf16[1024,288]{0,1:T(8,128)(2,1)}, u32[]{:S(2)}, u32[]{:S(2)}) %collective-permute-start.9) | collective-permute-done | bytes 589856 | tf_op jit(solution)/shard_map/ppermute | solution.py:236
  205.8 3.0 select_select_fusion.6
  210.6 12.0 %collective-permute-done.12 = bf16[1152,288]{0,1:T(8,128)(2,1)} collective-permute-done((bf16[1152,288]{0,1:T(8,128)(2,1)}, bf16[1152,288]{0,1:T(8,128)(2,1)}, u32[]{:S(2)}, u32[]{:S(2)}) %collective-permute-start.12) | collective-permute-done | bytes 663584 | tf_op jit(solution)/shard_map/ppermute | solution.py:236
  226.2 5.8 %concatenate.76 = bf16[1024,1152]{1,0:T(8,128)(2,1)} concatenate(bf16[1024,288]{1,0:T(8,128)(2,1)} %select_select_fusion.7, bf16[1024,288]{1,0:T(8,128)(2,1)} %select_select_fusion.6, bf16[1024,288]{1,0:T(8,128)(2,1)} %select_select_fusion.5, bf16[1024,288]{1,0:T(8,128)(2,1)} %select_select_fusion.4), dimensions={1} | concatenate | bytes 4718592 | tf_op jit(solution)/shard_map/concatenate | solution.py:317
  238.2 3.8 select_select_fusion
  242.0 6.3 %concatenate.78 = bf16[1152,1152]{1,0:T(8,128)(2,1)} concatenate(bf16[1152,288]{1,0:T(8,128)(2,1)} %get-tuple-element.46, bf16[1152,288]{1,0:T(8,128)(2,1)} %get-tuple-element.45, bf16[1152,288]{1,0:T(8,128)(2,1)} %get-tuple-element.44, bf16[1152,288]{1,0:T(8,128)(2,1)} %get-tuple-element.43), dimensions={1} | concatenate | bytes 5308416 | tf_op jit(solution)/shard_map/concatenate | solution.py:317
  248.3 6.1 %fusion.62 = (f32[1024]{0:T(1024)S(1)}, f32[1024,1152]{1,0:T(8,128)S(1)}) fusion(f32[1152]{0:T(1024)S(1)} %copy-done.40, bf16[1024,1152]{1,0:T(8,128)(2,1)} %concatenate.76, bf16[1152,1152]{1,0:T(8,128)(2,1)} %concatenate.78, bf16[1024,1152]{1,0:T(8,128)(2,1)S(1)} %constant_dynamic-update-slice_fusion.4), kind=kOutput, calls=%fused_computation.210 | convolution fusion | flops 2722626560 | bytes 12100096 | tf_op jit(solution)/shard_map/dot_general | solution.py:20
  259.1 4.1 convolution_add_fusion
  263.2 7.0 %convert_reduce_fusion.1 = (f32[1076]{0:T(1024)S(1)}, bf16[1024,1076]{0,1:T(8,128)(2,1)S(1)}) fusion(f32[1024,1076]{0,1:T(8,128)S(1)} %convolution_add_fusion, bf16[1024,1152]{1,0:T(8,128)(2,1)S(1)} %copy-done.33, bf16[1152,2440]{1,0:T(8,128)(2,1)S(1)} %bitcast.98), kind=kOutput, calls=%fused_computation.23 | convolution fusion | flops 2561739776 | bytes 11645136 | tf_op jit(solution)/shard_map/dot_general | solution.py:20
  270.2 4.5 fusion.63
  278.2 14.8 %collective-permute-done.29 = bf16[256,1152]{1,0:T(8,128)(2,1)S(1)} collective-permute-done((bf16[256,1152]{1,0:T(8,128)(2,1)S(1)}, bf16[256,1152]{1,0:T(8,128)(2,1)S(1)}, u32[]{:S(2)}, u32[]{:S(2)}) %collective-permute-start.29) | collective-permute-done | bytes 589856 | tf_op jit(solution)/shard_map/ppermute | solution.py:236
  297.5 12.7 %collective-permute-done.31 = bf16[256,1152]{1,0:T(8,128)(2,1)} collective-permute-done((bf16[256,1152]{1,0:T(8,128)(2,1)S(1)}, bf16[256,1152]{1,0:T(8,128)(2,1)}, u32[]{:S(2)}, u32[]{:S(2)}) %collective-permute-start.31) | collective-permute-done | bytes 589856 | tf_op jit(solution)/shard_map/ppermute | solution.py:236
  320.9 19.8 %attend_bwd.1 = bf16[1,1024,864]{2,1,0:T(8,128)(2,1)S(1)} custom-call(bf16[1,1024,864]{2,1,0:T(8,128)(2,1)S(1)} %copy-done.1, f32[1,1024,1]{2,1,0:T(8,128)S(1)} %fusion.41.bias_ref, f32[1,8,1024]{2,1,0:T(8,128)S(1)} %get-tuple-element.18.lse_ref, bf16[1,1024,288]{2,1,0:T(8,128)(2,1)S(1)} %fusion.20.grad_ref), custom_call_target="tpu_custom_call" | custom-call | flops 5368709120 | bytes 4423680 | tf_op jit(solution)/shard_map/attend_bwd/pallas_call | solution.py:121
  345.1 5.2 copy.196
  350.8 6.2 %convolution_convert_fusion = bf16[1152,1076]{0,1:T(8,128)(2,1)S(1)} fusion(bf16[1024,1076]{0,1:T(8,128)(2,1)} %copy-done.55, f32[1024,1152]{1,0:T(8,128)} %copy-done.6, f32[1152]{0:T(1024)S(1)} %copy-done.39, f32[1152]{0:T(1024)S(1)} %mul.267), kind=kOutput, calls=%fused_computation | convolution fusion | flops 2543380992 | bytes 9410560 | tf_op jit(solution)/shard_map/dot_general | solution.py:24
  357.1 5.8 %convolution_convert_fusion.1 = bf16[1152,1076]{0,1:T(8,128)(2,1)S(1)} fusion(bf16[1024,1152]{1,0:T(8,128)(2,1)S(1)} %copy-done.34, f32[1024,1076]{0,1:T(8,128)} %copy-done.56), kind=kOutput, calls=%fused_computation.1 | convolution fusion | flops 2549758464 | bytes 9245696 | tf_op jit(solution)/shard_map/dot_general | solution.py:24
  362.9 3.0 pad_maximum_fusion
  365.9 8.6 %copy.198 = bf16[1152,2152]{1,0:T(8,128)(2,1)} copy(bf16[1152,2152]{0,1:T(8,128)(2,1)} %pad_maximum_fusion) | data formatting | bytes 9916416
  374.5 10.5 %fusion.65 = (bf16[1024,1152]{1,0:T(8,128)(2,1)S(1)}, f32[1024,1152]{1,0:T(8,128)}) fusion(bf16[1152,2440]{1,0:T(8,128)(2,1)} %all-gather.5.cloned.1.call-done, f32[1024,1076]{0,1:T(8,128)} %copy-done.56), kind=kOutput, calls=%fused_computation.213 | convolution fusion | flops 2549698560 | bytes 14155776 | tf_op jit(solution)/shard_map/dot_general | solution.py:28
  396.5 4.5 fusion.64
  406.1 5.5 collective-permute-done.16
  414.8 3.2 collective-permute-start.17
  418.0 3.8 collective-permute-start.20
  426.4 17.2 %collective-permute-done.34 = bf16[256,1152]{1,0:T(8,128)(2,1)S(1)} collective-permute-done((bf16[256,1152]{1,0:T(8,128)(2,1)S(1)}, bf16[256,1152]{1,0:T(8,128)(2,1)S(1)}, u32[]{:S(2)}, u32[]{:S(2)}) %collective-permute-start.34) | collective-permute-done | bytes 589856 | tf_op jit(solution)/shard_map/ppermute | solution.py:236
  446.1 3.1 collective-permute-start.35
  449.2 42.8 %psum.15 = f32[1,13520]{1,0:T(1,128)S(1)} all-reduce(f32[1,13520]{1,0:T(1,128)S(1)} %broadcast_in_dim.155), channel_id=1, replica_groups=mesh['dev'=2,'z'=4,'y'=2,'core'=2] {'dev','z','y','core'}, use_global_device_ids=true, to_apply=%region_20.21 | all-reduce | flops 13520 | bytes 108160 | tf_op jit(solution)/shard_map/psum | solution.py:528
  493.2 4.2 collective-permute-start.37
  499.0 10.7 %collective-permute-done.37 = bf16[64,1152]{1,0:T(8,128)(2,1)S(1)} collective-permute-done((bf16[64,1152]{1,0:T(8,128)(2,1)S(1)}, bf16[64,1152]{1,0:T(8,128)(2,1)S(1)}, u32[]{:S(2)}, u32[]{:S(2)}) %collective-permute-start.37) | collective-permute-done | bytes 147488 | tf_op jit(solution)/shard_map/ppermute | solution.py:236
  509.7 9.8 %collective-permute-done.36 = bf16[64,1152]{1,0:T(8,128)(2,1)S(1)} collective-permute-done((bf16[64,1152]{1,0:T(8,128)(2,1)S(1)}, bf16[64,1152]{1,0:T(8,128)(2,1)S(1)}, u32[]{:S(2)}, u32[]{:S(2)}) %collective-permute-start.36) | collective-permute-done | bytes 147488 | tf_op jit(solution)/shard_map/ppermute | solution.py:236
  523.9 4.5 all-to-all-start.4
  529.9 3.4 all-to-all-start.5
  535.4 3.1 collective-permute-done.39
  541.4 4.4 all_to_all.134
  545.9 3.8 all-to-all-start.6
  (372 shorter events, 149.8 us)
Async XLA Ops:
  7.2 137.2 %all-gather.3.cloned.1.call-start = ((), (), s32[]{:S(2)}) async-start(), calls=%async_computation.10 | async-start | bytes 2322432 | tf_op jit(solution)/shard_map/all_gather | solution.py:424
  8.2 3.5 collective-permute-start.8
  21.2 104.6 %collective-permute-start.7 = (bf16[1,6760]{1,0:T(2,128)(2,1)S(1)}, bf16[1,6760]{1,0:T(2,128)(2,1)S(1)}, u32[]{:S(2)}, u32[]{:S(2)}) collective-permute-start(bf16[1,6760]{1,0:T(2,128)(2,1)S(1)} %concatenate.71), channel_id=1, source_target_pairs={{0,16},{1,17},{2,18},{3,19},{4,20},{5,21},{6,22},{7,23},{8,24},{9,... | collective-permute-start | bytes 40568 | tf_op jit(solution)/shard_map/ppermute | solution.py:236
  22.3 5.1 all-to-all-start.1
  26.3 174.9 %all-gather.5.cloned.1.call-start = ((), (), s32[]{:S(2)}) async-start(), calls=%async_computation.11 | async-start | bytes 6635520 | tf_op jit(solution)/shard_map/all_gather | solution.py:426
  36.9 485.2 %reduce-scatter.7.cloned.1.call-start = ((), (), s32[]{:S(2)}) async-start(), calls=%async_computation.12 | async-start | bytes 2985984 | tf_op jit(solution)/shard_map/reduce_scatter | solution.py:500
  37.1 62.8 %collective-permute-start.3 = (bf16[64,1152]{1,0:T(8,128)(2,1)S(1)}, bf16[64,1152]{1,0:T(8,128)(2,1)S(1)}, u32[]{:S(2)}, u32[]{:S(2)}) collective-permute-start(bf16[64,1152]{1,0:T(8,128)(2,1)S(1)} %get-tuple-element.77), channel_id=1, source_target_pairs={{0,12},{1,13},{2,28},{3,29},{4,0},{5,1},{6,16},{7,17},{8,4},{9,5},... | collective-permute-start | bytes 442376 | tf_op jit(solution)/shard_map/ppermute | solution.py:236
  39.2 54.8 %collective-permute-start.1 = (bf16[64,1152]{1,0:T(8,128)(2,1)S(1)}, bf16[64,1152]{1,0:T(8,128)(2,1)S(1)}, u32[]{:S(2)}, u32[]{:S(2)}) collective-permute-start(bf16[64,1152]{1,0:T(8,128)(2,1)S(1)} %get-tuple-element.78), channel_id=1, source_target_pairs={{0,4},{1,5},{2,20},{3,21},{4,8},{5,9},{6,24},{7,25},{8,12},{9,13},... | collective-permute-start | bytes 442376 | tf_op jit(solution)/shard_map/ppermute | solution.py:236
  40.4 50.8 %collective-permute-start = (bf16[64,1152]{1,0:T(8,128)(2,1)S(1)}, bf16[64,1152]{1,0:T(8,128)(2,1)S(1)}, u32[]{:S(2)}, u32[]{:S(2)}) collective-permute-start(bf16[64,1152]{1,0:T(8,128)(2,1)S(1)} %get-tuple-element.79), channel_id=1, source_target_pairs={{0,0},{1,1},{2,16},{3,17},{4,4},{5,5},{6,20},{7,21},{8,8},{9,9},{1... | collective-permute-start | bytes 442376 | tf_op jit(solution)/shard_map/ppermute | solution.py:236
  44.7 52.0 %collective-permute-start.2 = (bf16[64,1152]{1,0:T(8,128)(2,1)S(1)}, bf16[64,1152]{1,0:T(8,128)(2,1)S(1)}, u32[]{:S(2)}, u32[]{:S(2)}) collective-permute-start(bf16[64,1152]{1,0:T(8,128)(2,1)S(1)} %get-tuple-element.80), channel_id=1, source_target_pairs={{0,8},{1,9},{2,24},{3,25},{4,12},{5,13},{6,28},{7,29},{8,0},{9,1},... | collective-permute-start | bytes 442376 | tf_op jit(solution)/shard_map/ppermute | solution.py:236
  91.2 33.9 %collective-permute-start.24 = (bf16[64,1152]{1,0:T(8,128)(2,1)S(1)}, bf16[64,1152]{1,0:T(8,128)(2,1)S(1)}, u32[]{:S(2)}, u32[]{:S(2)}) collective-permute-start(bf16[64,1152]{1,0:T(8,128)(2,1)S(1)} %get-tuple-element.59), channel_id=1, source_target_pairs={{0,12},{1,13},{2,28},{3,29},{4,0},{5,1},{6,16},{7,17},{8,4},{9,5},... | collective-permute-start | bytes 442376 | tf_op jit(solution)/shard_map/ppermute | solution.py:236
  94.0 30.3 %collective-permute-start.23 = (bf16[64,1152]{1,0:T(8,128)(2,1)S(1)}, bf16[64,1152]{1,0:T(8,128)(2,1)S(1)}, u32[]{:S(2)}, u32[]{:S(2)}) collective-permute-start(bf16[64,1152]{1,0:T(8,128)(2,1)S(1)} %get-tuple-element.60), channel_id=1, source_target_pairs={{0,8},{1,9},{2,24},{3,25},{4,12},{5,13},{6,28},{7,29},{8,0},{9,1},... | collective-permute-start | bytes 442376 | tf_op jit(solution)/shard_map/ppermute | solution.py:236
  96.7 25.9 %collective-permute-start.22 = (bf16[64,1152]{1,0:T(8,128)(2,1)S(1)}, bf16[64,1152]{1,0:T(8,128)(2,1)S(1)}, u32[]{:S(2)}, u32[]{:S(2)}) collective-permute-start(bf16[64,1152]{1,0:T(8,128)(2,1)S(1)} %get-tuple-element.61), channel_id=1, source_target_pairs={{0,4},{1,5},{2,20},{3,21},{4,8},{5,9},{6,24},{7,25},{8,12},{9,13},... | collective-permute-start | bytes 442376 | tf_op jit(solution)/shard_map/ppermute | solution.py:236
  99.8 9.3 %collective-permute-start.21 = (bf16[64,1152]{1,0:T(8,128)(2,1)S(1)}, bf16[64,1152]{1,0:T(8,128)(2,1)S(1)}, u32[]{:S(2)}, u32[]{:S(2)}) collective-permute-start(bf16[64,1152]{1,0:T(8,128)(2,1)S(1)} %get-tuple-element.62), channel_id=1, source_target_pairs={{0,0},{1,1},{2,16},{3,17},{4,4},{5,5},{6,20},{7,21},{8,8},{9,9},{1... | collective-permute-start | bytes 442376 | tf_op jit(solution)/shard_map/ppermute | solution.py:236
  109.1 18.0 %collective-permute-start.5 = (bf16[256,1152]{1,0:T(8,128)(2,1)}, bf16[256,1152]{1,0:T(8,128)(2,1)S(1)}, u32[]{:S(2)}, u32[]{:S(2)}) collective-permute-start(bf16[256,1152]{1,0:T(8,128)(2,1)} %get-tuple-element.95), channel_id=1, source_target_pairs={{0,16},{1,17},{2,18},{3,19},{4,20},{5,21},{6,22},{7,23},{8,24},{9,... | collective-permute-start | bytes 1769480 | tf_op jit(solution)/shard_map/ppermute | solution.py:236
  122.6 19.2 %collective-permute-start.4 = (bf16[256,1152]{1,0:T(8,128)(2,1)}, bf16[256,1152]{1,0:T(8,128)(2,1)}, u32[]{:S(2)}, u32[]{:S(2)}) collective-permute-start(bf16[256,1152]{1,0:T(8,128)(2,1)} %get-tuple-element.95), channel_id=1, source_target_pairs={{0,1},{1,0},{2,3},{3,2},{4,5},{5,4},{6,7},{7,6},{8,9},{9,8},{10,11... | collective-permute-start | bytes 1769480 | tf_op jit(solution)/shard_map/ppermute | solution.py:236
  125.8 15.3 %collective-permute-start.26 = (bf16[256,1152]{1,0:T(8,128)(2,1)}, bf16[256,1152]{1,0:T(8,128)(2,1)}, u32[]{:S(2)}, u32[]{:S(2)}) collective-permute-start(bf16[256,1152]{1,0:T(8,128)(2,1)} %get-tuple-element.87), channel_id=1, source_target_pairs={{0,16},{1,17},{2,18},{3,19},{4,20},{5,21},{6,22},{7,23},{8,24},{9,... | collective-permute-start | bytes 1769480 | tf_op jit(solution)/shard_map/ppermute | solution.py:236
  127.0 16.0 %collective-permute-start.6 = (bf16[256,1152]{1,0:T(8,128)(2,1)S(1)}, bf16[256,1152]{1,0:T(8,128)(2,1)S(1)}, u32[]{:S(2)}, u32[]{:S(2)}) collective-permute-start(bf16[256,1152]{1,0:T(8,128)(2,1)S(1)} %collective-permute-done.5), channel_id=1, source_target_pairs={{0,1},{1,0},{2,3},{3,2},{4,5},{5,4},{6,7},{7,6},{8,9},{9,8},{10,11... | collective-permute-start | bytes 1769480 | tf_op jit(solution)/shard_map/ppermute | solution.py:236
  127.1 39.0 %collective-permute-start.25 = (bf16[256,1152]{1,0:T(8,128)(2,1)}, bf16[256,1152]{1,0:T(8,128)(2,1)}, u32[]{:S(2)}, u32[]{:S(2)}) collective-permute-start(bf16[256,1152]{1,0:T(8,128)(2,1)} %get-tuple-element.87), channel_id=1, source_target_pairs={{0,1},{1,0},{2,3},{3,2},{4,5},{5,4},{6,7},{7,6},{8,9},{9,8},{10,11... | collective-permute-start | bytes 1769480 | tf_op jit(solution)/shard_map/ppermute | solution.py:236
  141.1 38.5 %collective-permute-start.27 = (bf16[256,1152]{1,0:T(8,128)(2,1)}, bf16[256,1152]{1,0:T(8,128)(2,1)}, u32[]{:S(2)}, u32[]{:S(2)}) collective-permute-start(bf16[256,1152]{1,0:T(8,128)(2,1)} %collective-permute-done.26), channel_id=1, source_target_pairs={{0,1},{1,0},{2,3},{3,2},{4,5},{5,4},{6,7},{7,6},{8,9},{9,8},{10,11... | collective-permute-start | bytes 1769480 | tf_op jit(solution)/shard_map/ppermute | solution.py:236
  163.5 15.2 %collective-permute-start.9 = (bf16[1024,288]{0,1:T(8,128)(2,1)}, bf16[1024,288]{0,1:T(8,128)(2,1)}, u32[]{:S(2)}, u32[]{:S(2)}) collective-permute-start(bf16[1024,288]{0,1:T(8,128)(2,1)} %copy.148), channel_id=1, source_target_pairs={{0,16},{1,17},{2,18},{3,19},{4,20},{5,21},{6,22},{7,23},{8,24},{9,... | collective-permute-start | bytes 1769480 | tf_op jit(solution)/shard_map/ppermute | solution.py:236
  165.8 15.7 %collective-permute-start.11 = (bf16[1024,288]{0,1:T(8,128)(2,1)}, bf16[1024,288]{0,1:T(8,128)(2,1)S(1)}, u32[]{:S(2)}, u32[]{:S(2)}) collective-permute-start(bf16[1024,288]{0,1:T(8,128)(2,1)} %copy.148), channel_id=1, source_target_pairs={{0,1},{1,0},{2,3},{3,2},{4,5},{5,4},{6,7},{7,6},{8,9},{9,8},{10,11... | collective-permute-start | bytes 1769480 | tf_op jit(solution)/shard_map/ppermute | solution.py:236
  178.8 14.6 %collective-permute-start.10 = (bf16[1024,288]{0,1:T(8,128)(2,1)}, bf16[1024,288]{0,1:T(8,128)(2,1)}, u32[]{:S(2)}, u32[]{:S(2)}) collective-permute-start(bf16[1024,288]{0,1:T(8,128)(2,1)} %collective-permute-done.9), channel_id=1, source_target_pairs={{0,1},{1,0},{2,3},{3,2},{4,5},{5,4},{6,7},{7,6},{8,9},{9,8},{10,11... | collective-permute-start | bytes 1769480 | tf_op jit(solution)/shard_map/ppermute | solution.py:236
  205.7 16.9 %collective-permute-start.12 = (bf16[1152,288]{0,1:T(8,128)(2,1)}, bf16[1152,288]{0,1:T(8,128)(2,1)}, u32[]{:S(2)}, u32[]{:S(2)}) collective-permute-start(bf16[1152,288]{0,1:T(8,128)(2,1)} %copy.163), channel_id=1, source_target_pairs={{0,16},{1,17},{2,18},{3,19},{4,20},{5,21},{6,22},{7,23},{8,24},{9,... | collective-permute-start | bytes 1990664 | tf_op jit(solution)/shard_map/ppermute | solution.py:236
  210.3 23.2 %collective-permute-start.14 = (bf16[1152,288]{0,1:T(8,128)(2,1)}, bf16[1152,288]{0,1:T(8,128)(2,1)}, u32[]{:S(2)}, u32[]{:S(2)}) collective-permute-start(bf16[1152,288]{0,1:T(8,128)(2,1)} %copy.163), channel_id=1, source_target_pairs={{0,1},{1,0},{2,3},{3,2},{4,5},{5,4},{6,7},{7,6},{8,9},{9,8},{10,11... | collective-permute-start | bytes 1990664 | tf_op jit(solution)/shard_map/ppermute | solution.py:236
  222.7 13.2 %collective-permute-start.13 = (bf16[1152,288]{0,1:T(8,128)(2,1)}, bf16[1152,288]{0,1:T(8,128)(2,1)}, u32[]{:S(2)}, u32[]{:S(2)}) collective-permute-start(bf16[1152,288]{0,1:T(8,128)(2,1)} %collective-permute-done.12), channel_id=1, source_target_pairs={{0,1},{1,0},{2,3},{3,2},{4,5},{5,4},{6,7},{7,6},{8,9},{9,8},{10,11... | collective-permute-start | bytes 1990664 | tf_op jit(solution)/shard_map/ppermute | solution.py:236
  274.9 2.9 collective-permute-start.28
  278.1 14.9 %collective-permute-start.29 = (bf16[256,1152]{1,0:T(8,128)(2,1)S(1)}, bf16[256,1152]{1,0:T(8,128)(2,1)S(1)}, u32[]{:S(2)}, u32[]{:S(2)}) collective-permute-start(bf16[256,1152]{1,0:T(8,128)(2,1)S(1)} %fusion.23), channel_id=1, source_target_pairs={{0,16},{1,17},{2,18},{3,19},{4,20},{5,21},{6,22},{7,23},{8,24},{9,... | collective-permute-start | bytes 1769480 | tf_op jit(solution)/shard_map/ppermute | solution.py:236
  296.2 14.0 %collective-permute-start.31 = (bf16[256,1152]{1,0:T(8,128)(2,1)S(1)}, bf16[256,1152]{1,0:T(8,128)(2,1)}, u32[]{:S(2)}, u32[]{:S(2)}) collective-permute-start(bf16[256,1152]{1,0:T(8,128)(2,1)S(1)} %get-tuple-element.39), channel_id=1, source_target_pairs={{0,16},{1,17},{2,18},{3,19},{4,20},{5,21},{6,22},{7,23},{8,24},{9,... | collective-permute-start | bytes 1769480 | tf_op jit(solution)/shard_map/ppermute | solution.py:236
  296.2 18.8 %collective-permute-start.30 = (bf16[256,1152]{1,0:T(8,128)(2,1)S(1)}, bf16[256,1152]{1,0:T(8,128)(2,1)}, u32[]{:S(2)}, u32[]{:S(2)}) collective-permute-start(bf16[256,1152]{1,0:T(8,128)(2,1)S(1)} %get-tuple-element.39), channel_id=1, source_target_pairs={{0,1},{1,0},{2,3},{3,2},{4,5},{5,4},{6,7},{7,6},{8,9},{9,8},{10,11... | collective-permute-start | bytes 1769480 | tf_op jit(solution)/shard_map/ppermute | solution.py:236
  310.2 4.8 collective-permute-start.32
  350.4 189.1 %reduce-scatter.9.cloned.1.call-start = ((), (), s32[]{:S(2)}) async-start(), calls=%async_computation.13 | async-start | bytes 5640192 | tf_op jit(solution)/shard_map/reduce_scatter | solution.py:500
  388.2 3.2 collective-permute-start.15
  396.5 15.1 %collective-permute-start.16 = (bf16[256,1152]{1,0:T(8,128)(2,1)}, bf16[256,1152]{1,0:T(8,128)(2,1)}, u32[]{:S(2)}, u32[]{:S(2)}) collective-permute-start(bf16[256,1152]{1,0:T(8,128)(2,1)} %fusion.25), channel_id=1, source_target_pairs={{0,16},{1,17},{2,18},{3,19},{4,20},{5,21},{6,22},{7,23},{8,24},{9,... | collective-permute-start | bytes 1769480 | tf_op jit(solution)/shard_map/ppermute | solution.py:236
  402.3 21.8 %collective-permute-start.33 = (bf16[512,1152]{1,0:T(8,128)(2,1)}, bf16[512,1152]{1,0:T(8,128)(2,1)S(1)}, u32[]{:S(2)}, u32[]{:S(2)}) collective-permute-start(bf16[512,1152]{1,0:T(8,128)(2,1)} %pad_maximum_fusion.5), channel_id=1, source_target_pairs={{0,1},{1,0},{2,3},{3,2},{4,5},{5,4},{6,7},{7,6},{8,9},{9,8},{10,11... | collective-permute-start | bytes 3538952 | tf_op jit(solution)/shard_map/ppermute | solution.py:236
  414.8 77.2 %collective-permute-start.17 = (bf16[64,1152]{1,0:T(8,128)(2,1)}, bf16[64,1152]{1,0:T(8,128)(2,1)}, u32[]{:S(2)}, u32[]{:S(2)}) collective-permute-start(bf16[64,1152]{1,0:T(8,128)(2,1)} %get-tuple-element.63), channel_id=1, source_target_pairs={{0,0},{1,1},{2,16},{3,17},{4,4},{5,5},{6,20},{7,21},{8,8},{9,9},{1... | collective-permute-start | bytes 442376 | tf_op jit(solution)/shard_map/ppermute | solution.py:236
  418.0 75.2 %collective-permute-start.20 = (bf16[64,1152]{1,0:T(8,128)(2,1)S(1)}, bf16[64,1152]{1,0:T(8,128)(2,1)}, u32[]{:S(2)}, u32[]{:S(2)}) collective-permute-start(bf16[64,1152]{1,0:T(8,128)(2,1)S(1)} %get-tuple-element.64), channel_id=1, source_target_pairs={{0,4},{1,5},{2,20},{3,21},{4,8},{5,9},{6,24},{7,25},{8,12},{9,13},... | collective-permute-start | bytes 442376 | tf_op jit(solution)/shard_map/ppermute | solution.py:236
  421.9 75.5 %collective-permute-start.19 = (bf16[64,1152]{1,0:T(8,128)(2,1)S(1)}, bf16[64,1152]{1,0:T(8,128)(2,1)}, u32[]{:S(2)}, u32[]{:S(2)}) collective-permute-start(bf16[64,1152]{1,0:T(8,128)(2,1)S(1)} %get-tuple-element.65), channel_id=1, source_target_pairs={{0,8},{1,9},{2,24},{3,25},{4,12},{5,13},{6,28},{7,29},{8,0},{9,1},... | collective-permute-start | bytes 442376 | tf_op jit(solution)/shard_map/ppermute | solution.py:236
  422.0 77.0 %collective-permute-start.18 = (bf16[64,1152]{1,0:T(8,128)(2,1)S(1)}, bf16[64,1152]{1,0:T(8,128)(2,1)}, u32[]{:S(2)}, u32[]{:S(2)}) collective-permute-start(bf16[64,1152]{1,0:T(8,128)(2,1)S(1)} %get-tuple-element.66), channel_id=1, source_target_pairs={{0,12},{1,13},{2,28},{3,29},{4,0},{5,1},{6,16},{7,17},{8,4},{9,5},... | collective-permute-start | bytes 442376 | tf_op jit(solution)/shard_map/ppermute | solution.py:236
  425.7 17.9 %collective-permute-start.34 = (bf16[256,1152]{1,0:T(8,128)(2,1)S(1)}, bf16[256,1152]{1,0:T(8,128)(2,1)S(1)}, u32[]{:S(2)}, u32[]{:S(2)}) collective-permute-start(bf16[256,1152]{1,0:T(8,128)(2,1)S(1)} %fusion.21), channel_id=1, source_target_pairs={{0,16},{1,17},{2,18},{3,19},{4,20},{5,21},{6,22},{7,23},{8,24},{9,... | collective-permute-start | bytes 1769480 | tf_op jit(solution)/shard_map/ppermute | solution.py:236
  446.1 52.9 %collective-permute-start.35 = (bf16[64,1152]{1,0:T(8,128)(2,1)S(1)}, bf16[64,1152]{1,0:T(8,128)(2,1)S(1)}, u32[]{:S(2)}, u32[]{:S(2)}) collective-permute-start(bf16[64,1152]{1,0:T(8,128)(2,1)S(1)} %get-tuple-element.55), channel_id=1, source_target_pairs={{0,0},{1,1},{2,16},{3,17},{4,4},{5,5},{6,20},{7,21},{8,8},{9,9},{1... | collective-permute-start | bytes 442376 | tf_op jit(solution)/shard_map/ppermute | solution.py:236
  492.0 7.1 %collective-permute-start.38 = (bf16[64,1152]{1,0:T(8,128)(2,1)S(1)}, bf16[64,1152]{1,0:T(8,128)(2,1)S(1)}, u32[]{:S(2)}, u32[]{:S(2)}) collective-permute-start(bf16[64,1152]{1,0:T(8,128)(2,1)S(1)} %get-tuple-element.56), channel_id=1, source_target_pairs={{0,4},{1,5},{2,20},{3,21},{4,8},{5,9},{6,24},{7,25},{8,12},{9,13},... | collective-permute-start | bytes 442376 | tf_op jit(solution)/shard_map/ppermute | solution.py:236
  493.2 16.5 %collective-permute-start.37 = (bf16[64,1152]{1,0:T(8,128)(2,1)S(1)}, bf16[64,1152]{1,0:T(8,128)(2,1)S(1)}, u32[]{:S(2)}, u32[]{:S(2)}) collective-permute-start(bf16[64,1152]{1,0:T(8,128)(2,1)S(1)} %get-tuple-element.57), channel_id=1, source_target_pairs={{0,8},{1,9},{2,24},{3,25},{4,12},{5,13},{6,28},{7,29},{8,0},{9,1},... | collective-permute-start | bytes 442376 | tf_op jit(solution)/shard_map/ppermute | solution.py:236
  497.4 22.2 %collective-permute-start.36 = (bf16[64,1152]{1,0:T(8,128)(2,1)S(1)}, bf16[64,1152]{1,0:T(8,128)(2,1)S(1)}, u32[]{:S(2)}, u32[]{:S(2)}) collective-permute-start(bf16[64,1152]{1,0:T(8,128)(2,1)S(1)} %get-tuple-element.58), channel_id=1, source_target_pairs={{0,12},{1,13},{2,28},{3,29},{4,0},{5,1},{6,16},{7,17},{8,4},{9,5},... | collective-permute-start | bytes 442376 | tf_op jit(solution)/shard_map/ppermute | solution.py:236
  523.9 6.0 %all-to-all-start.4 = ((bf16[2,72,864]{2,1,0:T(8,128)(2,1)}), bf16[2,72,864]{2,1,0:T(8,128)(2,1)S(1)}, u32[]{:S(2)}, u32[]{:S(2)}) async-start(bf16[2,72,864]{2,1,0:T(8,128)(2,1)} %bitcast.25), calls=%async_computation.4 | async-start | bytes 516096 | tf_op jit(solution)/shard_map/all_to_all | solution.py:343
  529.9 4.5 all-to-all-start.5
  534.2 4.3 collective-permute-start.39
  545.9 5.5 all-to-all-start.6
  (63 other events, 1059.8 us)
Sparse Core Ops, SparseCore 0:
  21.1 56.4 all-gather.2
  79.8 103.8 all-gather.4
  350.5 69.2 reduce-scatter.6
  423.8 108.1 reduce-scatter.8
